TPU v7x, 32 devices: a whole 2x2x4 slice. The times are simulated.
32 devices in a mesh: tile: 16 (over z, x, core), group: 2 (over y).
Axes of the slice: x: 2, y: 2, z: 4, core: 2. Of those that a mesh axis runs over, the one named last changes fastest.
Arguments:
- object_field: float32 [2, 320, 2048], P(None, 'group', 'tile'), may hold values from -6 to 6
- probe_field: float32 [2, 256, 256], replicated, may hold values from -6 to 6
- amplitudes: float32 [32, 256, 256], P(('tile', 'group')), may hold values from 0 to 4
- row_start: int32 [32], P(('tile', 'group')), may hold values from 0 to 64
- column_start: int32 [32], P(('tile', 'group')), may hold values from 0 to 128
- live_slots: int32 [32], P(('tile', 'group')), may hold values 0 or 1
Outputs:
- new_object: float32 [2, 320, 2048], P(None, 'group', 'tile')
- new_probe: float32 [2, 256, 256], replicated
All inputs are finite; a program needn't handle non-finite values. No bound on the sum of `live_slots` on one device may be relied on, other than what follows from the above.
Results may differ from a plain program's by a relative error of at most 0.0001.
Values sent between devices are 32-bit elements; how exact they have to be, the bound alone decides.
A program may use at most 64 MiB of HBM per device.

v0:
```python
import functools
import math

import jax
import jax.numpy as jnp
import numpy as np
from jax import lax
from jax.experimental import pallas as pl
from jax.experimental.pallas import tpu as pltpu
from jax.sharding import PartitionSpec as P

MESH = pl.DeviceIdType.MESH
F32 = jnp.float32
BF16 = jnp.bfloat16


def dft_tables(length):
    k = np.arange(length)
    angles = 2.0 * math.pi / length * (np.outer(k, k) % length)
    cos, sin = np.cos(angles) / math.sqrt(length), np.sin(angles) / math.sqrt(length)
    full = np.block([[cos, sin], [-sin, cos]]).astype(np.float32)
    head = full.astype(BF16)
    tail = (full - head.astype(np.float32)).astype(BF16)
    return head, tail


def split(x):
    head = x.astype(BF16)
    return head, (x - head.astype(F32)).astype(BF16)


def mm(a, b):
    return jnp.dot(a, b, preferred_element_type=F32)


def table_left(head, tail, x):
    xh, xl = split(x)
    return mm(head, xh) + (mm(head, xl) + mm(tail, xh))


def table_right(x, head, tail):
    xh, xl = split(x)
    return mm(xh, head) + (mm(xl, head) + mm(xh, tail))


def remote(src, dst, send, recv, tile, group):
    return pltpu.make_async_remote_copy(
        src_ref=src, dst_ref=dst, send_sem=send, recv_sem=recv,
        device_id={"tile": tile, "group": group}, device_id_type=MESH,
    )


class AllReduce:
    def __init__(self, plan, part, pair, mine, came, full, sems):
        self.p, self.part, self.pair, self.mine = plan, part, pair, mine
        self.came, self.full, self.sems = came, full, sems

    def pair_copy(self):
        p = self.p
        return remote(self.part.at[1 - p.h, p.s], self.pair, self.sems[0].at[0],
                      self.sems[1].at[0], p.partner, p.g)

    def spread_copy(self, d):
        p = self.p
        to = lax.rem(p.k + d, p.H)
        return remote(self.mine.at[to], self.came.at[d - 1], self.sems[2].at[d - 1],
                      self.sems[3].at[d - 1], 2 * to + p.h, p.g)

    def collect_copy(self, dg, dk, arriving):
        p = self.p
        n = dg * p.H + dk
        sign = -1 if arriving else 1
        if dg == 0:
            k = lax.rem(p.k + sign * dk + p.H, p.H)
            slot = self.full.at[p.h, p.s, k if arriving else p.k]
            to, group = 2 * k + p.h, p.g
        else:
            s = lax.rem(p.s + sign * dg + p.gs, p.gs)
            slot = self.full.at[p.h, s if arriving else p.s, lax.rem(p.k - dk + p.H, p.H)]
            to, group = 2 * p.k + p.h, p.g - p.s + s
        return remote(slot, slot, self.sems[4].at[n], self.sems[5].at[n], to, group)

    def relay_copy(self, dg, dk, arriving):
        p = self.p
        n = dg * p.H + dk
        k = lax.rem(p.k - dk + p.H, p.H)
        s = lax.rem(p.s - dg + p.gs, p.gs)
        h = 1 - p.h if arriving else p.h
        slot = self.full.at[h, s, k]
        return remote(slot, slot, self.sems[6].at[n], self.sems[7].at[n], p.partner, p.g)

    def others(self):
        p = self.p
        return [(dg, dk) for dk in range(p.H) for dg in range(p.gs) if dg or dk]

    def put(self, channel, value):
        p = self.p
        self.part[:, :, :, channel] = value.reshape(2, p.gs, p.H, p.rows, value.shape[-1])

    def start_pair(self):
        self.pair_copy().start()

    def start_spread(self):
        p = self.p
        self.pair_copy().wait()
        self.mine[...] = self.part[p.h, p.s] + self.pair[...]
        for d in range(1, p.H):
            self.spread_copy(d).start()

    def start_collect(self):
        p = self.p
        total = self.mine[p.k]
        for d in range(1, p.H):
            self.spread_copy(d).wait()
            total = total + self.came[d - 1]
        self.full[p.h, p.s, p.k] = total
        for dk in range(1, p.H):
            self.collect_copy(0, dk, False).start()
        for dg in range(1, p.gs):
            self.collect_copy(dg, 0, False).start()
        self.relay_copy(0, 0, False).start()

    def relay(self):
        p = self.p
        for dk in range(p.H):
            if dk > 0:
                self.collect_copy(0, dk, True).wait_recv()
                for dg in range(1, p.gs):
                    self.collect_copy(dg, dk, False).start()
                self.relay_copy(0, dk, False).start()
        for dk in range(p.H):
            for dg in range(1, p.gs):
                self.collect_copy(dg, dk, True).wait_recv()
                self.relay_copy(dg, dk, False).start()

    def finish(self):
        self.relay_copy(0, 0, True).wait_recv()
        self.relay_copy(0, 0, False).wait_send()
        for dg, dk in self.others():
            self.relay_copy(dg, dk, True).wait_recv()
            self.relay_copy(dg, dk, False).wait_send()
            self.collect_copy(dg, dk, False).wait_send()

    def get(self, channel):
        whole = self.full[:, :, :, channel]
        return whole.reshape(-1, whole.shape[-1])


class Plan:
    pass


def kernel(T, G, gs, row_in, column_in, live_in, obj, probe_in, amp, *args):
    tables_in, args = args[:4], args[4:]
    (new_obj, new_probe, scal_in, probe, *args) = args
    (a_head, a_tail, b_head, b_tail, load_sem, far), args = args[:6], args[6:]
    body(T, G, gs, (row_in, column_in, live_in), (obj, probe_in, amp, *tables_in),
         (probe, a_head, a_tail, b_head, b_tail), load_sem, far, scal_in, probe, a_head, a_tail,
         b_head, b_tail, new_obj, new_probe, *args)


def body(T, G, gs, scalars, inputs, loaded, load_sem, far, scal_in, probe, a_head, a_tail, b_head,
         b_tail, new_obj, new_probe, pad, amps, scal_all, win, terms, light_terms, acc, acc_light,
           edge, edge_light, grad_sum, *rest):
    t, g = lax.axis_index("tile"), lax.axis_index("group")
    obj, probe_in, amp, *tables_in = inputs
    R, W = obj.shape[1], probe.shape[1]
    B = obj.shape[2]
    rows = pad.shape[2]
    p = Plan()
    p.g, p.H, p.gs = g, T // 2, gs
    p.k, p.h = lax.div(t, 2), lax.rem(t, 2)
    p.partner = t + 1 - 2 * p.h
    p.s = lax.rem(g, gs)
    p.rows = W // 2 // (p.H * gs)
    light_red = AllReduce(p, *rest[0:5], rest[5:13])
    grad_red = AllReduce(p, *rest[13:18], rest[18:26])
    (own_s, own_r, side_s, side_r, amp_s, amp_r, scal_s, scal_r,
     edge_s, edge_r) = rest[26:36]

    own = pad.at[1, :, pl.ds(pl.multiple_of(g * R, 8), R)]
    loads = [pltpu.make_async_copy(src, dst, load_sem.at[i]) for i, (src, dst) in enumerate(
        [(obj, own), (amp.at[0], amps.at[g]), *zip((probe_in, *tables_in), loaded)])]
    for load in loads:
        load.start()
    barrier = pltpu.get_barrier_semaphore()
    count = 0
    for dt in range(T):
        for dg in range(G):
            if (dt or dg) and (dt == 0 or (dt % 2 == 0 and dg == 0)):
                pl.semaphore_signal(
                    barrier, inc=1,
                    device_id={"tile": lax.rem(t + dt, T), "group": lax.rem(g + dg, G)},
                    device_id_type=MESH)
                count += 1
    for to, there in ((t - 1, t > 0), (t + 1, t < T - 1)):
        @pl.when(there)
        def _():
            pl.semaphore_signal(barrier, inc=1, device_id={"tile": to, "group": g}, device_id_type=MESH)
    scal = scal_all
    line = lax.broadcasted_iota(jnp.int32, scal_in.shape, 0)
    scal_in[...] = jnp.where(line == 0, scalars[0][0], jnp.where(line == 1, scalars[1][0], scalars[2][0]))
    edges_here = (t > 0).astype(jnp.int32) + (t < T - 1).astype(jnp.int32)
    pl.semaphore_wait(barrier, count + edges_here)
    loads[0].wait()
    loads[1].wait()

    def span(group):
        return pl.ds(pl.multiple_of(group * R, 8), R)

    def to_peer(j, ch, arriving):
        peer = lax.rem(g + (G - j if arriving else j), G)
        slot = pad.at[1, ch, span(peer if arriving else g)]
        n = 2 * (j - 1) + ch
        return remote(slot, slot, own_s.at[n], own_r.at[n], t, peer)

    def to_side(j, ch, right, arriving):
        who = lax.rem(g + G - j, G)
        block = (0 if right else 2)
        dst = pad.at[block, ch, span(who)]
        src = pad.at[1, ch, span(who)]
        n = 4 * j + 2 * ch + int(right)
        return remote(dst if arriving else src, dst, side_s.at[n], side_r.at[n],
                      (t + 1 if right else t - 1) if not arriving else (t - 1 if right else t + 1), g)

    def amp_copy(j, arriving):
        peer = lax.rem(g + (G - j if arriving else j), G)
        slot = amps.at[peer if arriving else g]
        return remote(slot, slot, amp_s.at[j - 1], amp_r.at[j - 1], t, peer)

    def scal_copy(j, arriving):
        peer = lax.rem(g + (G - j if arriving else j), G)
        slot = scal.at[peer if arriving else g]
        return remote(slot if arriving else scal_in, slot, scal_s.at[j - 1], scal_r.at[j - 1], t, peer)

    def edge_copy(src, dst, right, base, arriving):
        n = base + int(right)
        side = dst.at[0 if right else 1]
        if arriving:
            return remote(side, side, edge_s.at[n], edge_r.at[n], t - 1 if right else t + 1, g)
        return remote(src.at[2 if right else 0], side, edge_s.at[n], edge_r.at[n],
                      t + 1 if right else t - 1, g)

    not_first, not_last = t > 0, t < T - 1

    for ch in range(2):
        for j in range(1, G):
            to_peer(j, ch, False).start()
    for ch in range(2):
        pl.when(not_first)(lambda: to_side(0, ch, False, False).start())
        pl.when(not_last)(lambda: to_side(0, ch, True, False).start())
    for j in range(1, G):
        scal_copy(j, False).start()
    for j in range(1, G):
        amp_copy(j, False).start()

    scal[g] = scal_in[...]

    @pl.when(t == 0)
    def _():
        pad[0] = jnp.zeros(pad.shape[1:], F32)
        edge[0] = jnp.zeros(edge.shape[1:], F32)
        edge_light[0] = jnp.zeros(edge_light.shape[1:], F32)

    @pl.when(t == T - 1)
    def _():
        pad[2] = jnp.zeros(pad.shape[1:], F32)
        edge[1] = jnp.zeros(edge.shape[1:], F32)
        edge_light[1] = jnp.zeros(edge_light.shape[1:], F32)

    spare = rows - W
    blocks = W // B
    terms[:, :, 0:spare] = jnp.zeros((2, blocks, spare, B), F32)
    terms[:, :, spare + W:] = jnp.zeros((2, blocks, spare, B), F32)
    light_terms[:, 0:spare] = jnp.zeros((blocks, spare, B), F32)
    light_terms[:, spare + W:] = jnp.zeros((blocks, spare, B), F32)

    def hold(ref, value):
        for b in range(blocks):
            ref[b, spare:spare + W] = value[:, b * B:(b + 1) * B]

    for load in loads[2:]:
        load.wait()
    probe_light = probe[0] * probe[0] + probe[1] * probe[1]
    hold(light_terms, probe_light)
    light_max = jnp.max(probe_light) + 1e-06

    for ch in range(2):
        for j in range(1, G):
            to_peer(j, ch, True).wait_recv()
            pl.when(not_first)(lambda: to_side(j, ch, False, False).start())
            pl.when(not_last)(lambda: to_side(j, ch, True, False).start())
    for j in range(1, G):
        scal_copy(j, True).wait_recv()
    for j in range(G):
        for ch in range(2):
            pl.when(not_last)(lambda: to_side(j, ch, False, True).wait_recv())
            pl.when(not_first)(lambda: to_side(j, ch, True, True).wait_recv())

    def numbers(k):
        return scal[k, 0, 0], scal[k, 1, 0], scal[k, 2, 0].astype(F32)

    def placed(ref, row, column):
        first = g * R + spare - row
        pieces = [ref[b, pl.ds(first, R), :] for b in range(blocks)]
        wide = jnp.concatenate(pieces + [jnp.zeros((R, 3 * B - W), F32)], axis=1)
        return pltpu.roll(wide, column, 1)

    acc[...] = jnp.zeros(acc.shape, F32)
    acc_light[...] = jnp.zeros(acc_light.shape, F32)
    grad_sum[...] = jnp.zeros(grad_sum.shape, F32)

    def look(j, light):
        k = lax.rem(g + j, G)
        row, column, weight = numbers(k)
        for ch in range(2):
            wide = jnp.concatenate([pad[b, ch, pl.ds(row, W), :] for b in range(3)], axis=1)
            win[k, ch] = pltpu.roll(wide, lax.rem(3 * B - column, 3 * B), 1)[:, 0:W]
        spread = weight * placed(light_terms, row, column)
        for b in range(3):
            acc_light[b] += spread[:, b * B:(b + 1) * B]
        return light + weight * (win[k, 0] * win[k, 0] + win[k, 1] * win[k, 1])

    light = lax.fori_loop(0, G, look, jnp.zeros((W, W), F32))
    light_red.put(0, light)
    light_red.start_pair()
    pl.when(not_first)(lambda: edge_copy(acc_light, edge_light, False, 0, False).start())
    pl.when(not_last)(lambda: edge_copy(acc_light, edge_light, True, 0, False).start())

    def forth(k):
        wr, wi = win[k, 0], win[k, 1]
        pr, pi = probe[0], probe[1]
        x = jnp.concatenate([pr * wr - pi * wi, pr * wi + pi * wr], axis=0)
        y = table_left(a_head[...], a_tail[...], x)
        z = table_right(jnp.concatenate([y[:W], y[W:]], axis=1), b_head[...], b_tail[...])
        zr, zi = z[:, :W], z[:, W:]
        factor = 1.0 - amps[k] * lax.rsqrt(jnp.maximum(zr * zr + zi * zi, 0.0625))
        far[0:W], far[W:] = zr * factor, zi * factor

    def back(k):
        row, column, weight = numbers(k)
        wr, wi = win[k, 0], win[k, 1]
        pr, pi = probe[0], probe[1]
        x = far[...]
        y = table_left(b_head[...], b_tail[...], x)
        z = table_right(jnp.concatenate([y[:W], y[W:]], axis=1), a_head[...], a_tail[...])
        mr, mi = z[:, :W] * weight, z[:, W:] * weight
        hold(terms.at[0], pr * mr + pi * mi)
        hold(terms.at[1], pr * mi - pi * mr)
        grad_sum[0] += wr * mr + wi * mi
        grad_sum[1] += wr * mi - wi * mr
        for ch in range(2):
            spread = placed(terms.at[ch], row, column)
            for b in range(3):
                acc[b, ch] += spread[:, b * B:(b + 1) * B]

    forth(g)
    light_red.start_spread()
    back(g)
    for j in range(1, G):
        amp_copy(j, True).wait_recv()

    def both(j):
        back(lax.rem(g + j, G))
        forth(lax.rem(g + j + 1, G))

    if G > 1:
        forth(lax.rem(g + 1, G))
        light_red.start_collect()
        pl.loop(1, G - 1)(both)
        back(lax.rem(g + G - 1, G))
    else:
        light_red.start_collect()

    for ch in range(2):
        grad_red.put(ch, grad_sum[ch])
    grad_red.start_pair()
    pl.when(not_first)(lambda: edge_copy(acc, edge, False, 2, False).start())
    pl.when(not_last)(lambda: edge_copy(acc, edge, True, 2, False).start())
    grad_red.start_spread()
    light_red.relay()
    grad_red.start_collect()

    for src, dst, base in ((acc_light, edge_light, 0), (acc, edge, 2)):
        pl.when(not_last)(lambda: edge_copy(src, dst, False, base, True).wait_recv())
        pl.when(not_first)(lambda: edge_copy(src, dst, True, base, True).wait_recv())
    below = 1.0 / (acc_light[1] + edge_light[0] + edge_light[1] + 0.25 * light_max)
    for ch in range(2):
        new_obj[ch] = own[ch] - (acc[1, ch] + edge[0, ch] + edge[1, ch]) * below
    light_red.finish()
    light = light_red.get(0)
    below = 1.0 / (light + 0.25 * jnp.mean(light) + 1e-05)
    grad_red.relay()
    grad_red.finish()
    for ch in range(2):
        new_probe[ch] = probe[ch] - grad_red.get(ch) * below

    for j in range(1, G):
        for ch in range(2):
            to_peer(j, ch, False).wait_send()
        amp_copy(j, False).wait_send()
        scal_copy(j, False).wait_send()
    for j in range(G):
        for ch in range(2):
            pl.when(not_first)(lambda: to_side(j, ch, False, False).wait_send())
            pl.when(not_last)(lambda: to_side(j, ch, True, False).wait_send())
    for src, dst, base in ((acc_light, edge_light, 0), (acc, edge, 2)):
        pl.when(not_first)(lambda: edge_copy(src, dst, False, base, False).wait_send())
        pl.when(not_last)(lambda: edge_copy(src, dst, True, base, False).wait_send())


def put(obj, probe, obj_out, probe_out, sems):
    copies = [pltpu.make_async_copy(obj, obj_out, sems.at[0]),
              pltpu.make_async_copy(probe, probe_out, sems.at[1])]
    for copy in copies:
        copy.start()
    for copy in copies:
        copy.wait()


def local(T, G, object_field, probe_field, amplitudes, row_start, column_start, live_slots):
    R, B = object_field.shape[1:]
    W = probe_field.shape[1]
    rows = R * G
    H = T // 2
    gs = max(n for n in range(1, G + 1) if G % n == 0 and n * H * 8 <= W // 2)
    chunk = W // 2 // (H * gs)
    head, tail = dft_tables(W)
    spare = rows - W
    dma = lambda n: pltpu.SemaphoreType.DMA((max(n, 1),))

    def reduce_scratch(channels):
        return [
            pltpu.VMEM((2, gs, H, channels, chunk, W), F32),
            pltpu.VMEM((H, channels, chunk, W), F32),
            pltpu.VMEM((H, channels, chunk, W), F32),
            pltpu.VMEM((H - 1, channels, chunk, W), F32),
            pltpu.VMEM((2, gs, H, channels, chunk, W), F32),
            dma(1), dma(1), dma(H - 1), dma(H - 1), dma(gs * H), dma(gs * H), dma(gs * H), dma(gs * H),
        ]

    vmem_limit = 67043328 - 4 * (object_field.size + probe_field.size) - 65536
    smem = pl.BlockSpec(memory_space=pltpu.SMEM)
    hbm = pl.BlockSpec(memory_space=pltpu.HBM)
    vmem = pl.BlockSpec(memory_space=pltpu.VMEM)
    new_obj, new_probe = pl.pallas_call(
        functools.partial(kernel, T, G, gs),
        out_shape=(pltpu.VMEM(object_field.shape, F32), pltpu.VMEM(probe_field.shape, F32)),
        in_specs=[smem] * 3 + [hbm] * 7,
        out_specs=(vmem, vmem),
        scratch_shapes=[
            pltpu.VMEM((8, 128), jnp.int32),
            pltpu.VMEM(probe_field.shape, F32),
            *[pltpu.VMEM(head.shape, BF16)] * 4,
            dma(7),
            pltpu.VMEM((2 * W, W), F32),
            pltpu.VMEM((3, 2, rows, B), F32),
            pltpu.VMEM((G, W, W), F32),
            pltpu.VMEM((G, 8, 128), jnp.int32),
            pltpu.VMEM((G, 2, W, W), F32),
            pltpu.VMEM((2, W // B, W + 2 * spare, B), F32),
            pltpu.VMEM((W // B, W + 2 * spare, B), F32),
            pltpu.VMEM((3, 2, R, B), F32),
            pltpu.VMEM((3, R, B), F32),
            pltpu.VMEM((2, 2, R, B), F32),
            pltpu.VMEM((2, R, B), F32),
            pltpu.VMEM((2, W, W), F32),
            *reduce_scratch(1),
            *reduce_scratch(2),
            dma(2 * G - 2), dma(2 * G - 2), dma(4 * G), dma(4 * G), dma(G - 1), dma(G - 1),
            dma(G - 1), dma(G - 1), dma(4), dma(4),
        ],
        compiler_params=pltpu.CompilerParams(
            collective_id=0, has_side_effects=True, vmem_limit_bytes=vmem_limit),
    )(row_start, column_start, live_slots, object_field, probe_field, amplitudes, head, tail,
      head.T, tail.T)
    anywhere = pl.BlockSpec(memory_space=pl.ANY)
    return pl.pallas_call(
        put,
        out_shape=(jax.ShapeDtypeStruct(object_field.shape, F32),
                   jax.ShapeDtypeStruct(probe_field.shape, F32)),
        in_specs=[vmem] * 2,
        out_specs=(anywhere, anywhere),
        scratch_shapes=[dma(2)],
        compiler_params=pltpu.CompilerParams(vmem_limit_bytes=1024 * 1024),
    )(new_obj, new_probe)


def solution(mesh):
    return jax.shard_map(
        functools.partial(local, mesh.shape["tile"], mesh.shape["group"]),
        mesh=mesh,
        in_specs=(
            P(None, "group", "tile"),
            P(),
            P(("tile", "group"), None, None),
            P(("tile", "group")),
            P(("tile", "group")),
            P(("tile", "group")),
        ),
        out_specs=(P(None, "group", "tile"), P()),
        check_vma=False,
    )
```

profile of v0, /device:TPU:0, one launch (start us, length us, event | category | flops | bytes accessed | tf_op | source)
XLA Modules:
  0.0 45.0 jit_solution(3763735085137760261)
XLA Ops:
  2.6 41.6 %shard_map.113 = (f32[2,160,128]{2,1,0:T(8,128)S(1)}, f32[2,256,256]{2,1,0:T(8,128)S(1)}) custom-call(s32[1]{0:T(128)S(6)} %copy.12.row_in, s32[1]{0:T(128)S(6)} %copy.13.column_in, s32[1]{0:T(128)S(6)} %copy.14.live_in, f32[2,160,128]{2,1,0:T(8,128)} %obj.1, f32[2,256,256]{2,1,0:T(8,128)} %probe_in.1, f32[1,256,256]{2,1,0:T(8,128)} %amp.1, ...), custom_call_target="tpu_custom_call" | custom-call | tf_op jit(solution)/shard_map/pallas_call | solution.py:446
  44.1 0.9 %shard_map.114 = (f32[2,160,128]{2,1,0:T(8,128)}, f32[2,256,256]{2,1,0:T(8,128)}) custom-call(f32[2,160,128]{2,1,0:T(8,128)S(1)} %get-tuple-element.4.obj, f32[2,256,256]{2,1,0:T(8,128)S(1)} %get-tuple-element.5.probe), custom_call_target="tpu_custom_call" | custom-call | tf_op jit(solution)/shard_map/pallas_call | solution.py:478
where the time goes:
time: 45.2 us; the launch traced here: 45 us
  Pallas kernels  42.4 us (94%)
  between operations  2.58 us (6%)
    pallas_call x1, Pallas kernels, local(): pl.pallas_call(functools.partial(kernel, T, G, gs), out_shape=(pltpu.VMEM...  41.6 us

commit v1 on v0

v1 whole, which is shorter than its diff:
```python
import functools
import math

import jax
import jax.numpy as jnp
import numpy as np
from jax import lax
from jax.experimental import pallas as pl
from jax.experimental.pallas import tpu as pltpu
from jax.sharding import PartitionSpec as P

MESH = pl.DeviceIdType.MESH
F32 = jnp.float32
BF16 = jnp.bfloat16


def dft_tables(length):
    k = np.arange(length // 2)
    even = (2 * np.outer(k, k)) % length
    odd = np.outer(2 * k + 1, k) % length
    tables = []
    for turns in (even, odd):
        angles = 2.0 * math.pi / length * turns
        cos, sin = np.cos(angles) / math.sqrt(length), np.sin(angles) / math.sqrt(length)
        full = np.block([[cos, sin], [-sin, cos]])
        tables += [full, full.T]
    full = np.stack(tables).astype(np.float32)
    head = full.astype(BF16)
    tail = (full - head.astype(np.float32)).astype(BF16)
    return np.stack([head, tail], axis=1)


EVEN, EVEN_T, ODD, ODD_T = range(4)


def split(x):
    head = x.astype(BF16)
    return head, (x - head.astype(F32)).astype(BF16)


def mm(a, b):
    return jnp.dot(a, b, preferred_element_type=F32)


def cat(parts, axis):
    return jnp.concatenate(parts, axis=axis)


def table_left(table, x):
    head, tail = split(x)
    return mm(cat([table[0], table[0], table[1]], 1), cat([head, tail, head], 0))


def table_right(x, table):
    head, tail = split(x)
    return mm(cat([head, tail, head], 1), cat([table[0], table[0], table[1]], 0))


def fold_in(xr, xi, tables):
    n = xr.shape[0] // 2
    a = cat([xr[:n] + xr[n:], xi[:n] + xi[n:]], 0)
    b = cat([xr[:n] - xr[n:], xi[:n] - xi[n:]], 0)
    halves = table_left(tables[EVEN], a), table_left(tables[ODD], b)

    def sides(sign):
        rows = []
        for y in halves:
            yr, yi = y[:n], y[n:]
            rows.append(cat([yr[:, :n] + sign * yr[:, n:], yi[:, :n] + sign * yi[:, n:]], 1))
        return cat(rows, 0)

    return table_right(sides(1), tables[EVEN_T]), table_right(sides(-1), tables[ODD_T])


def fold_out(even, odd, tables):
    n = even.shape[0] // 2
    e, o = table_right(even, tables[EVEN]), table_right(odd, tables[ODD])
    plus, minus = e + o, e - o
    halves = []
    for q, table in ((0, tables[EVEN_T]), (1, tables[ODD_T])):
        r = slice(q * n, (q + 1) * n)
        halves.append(table_left(table, cat(
            [cat([plus[r, :n], minus[r, :n]], 1), cat([plus[r, n:], minus[r, n:]], 1)], 0)))
    plus, minus = halves[0] + halves[1], halves[0] - halves[1]
    return cat([plus[:n], minus[:n]], 0), cat([plus[n:], minus[n:]], 0)


def remote(src, dst, send, recv, tile, group):
    return pltpu.make_async_remote_copy(
        src_ref=src, dst_ref=dst, send_sem=send, recv_sem=recv,
        device_id={"tile": tile, "group": group}, device_id_type=MESH,
    )


class Plan:
    def __init__(self, T, G, W):
        self.H = T // 2
        self.owners = self.H // 2 if self.H % 4 == 0 else self.H
        self.first = (self.H - self.owners) // 2
        self.gs = max(n for n in range(1, G + 1) if G % n == 0 and n * self.owners * 8 <= W // 2)
        self.W, self.half = W, W // 2
        self.part = self.half // self.gs
        self.chunk = self.part // self.owners

    def here(self, t, g):
        self.t, self.g = t, g
        self.k, self.h = lax.div(t, 2), lax.rem(t, 2)
        self.partner = t + 1 - 2 * self.h
        self.s = lax.rem(g, self.gs)
        self.mine = self.k - self.first
        self.low = self.k < self.H // 2
        self.owner = jnp.logical_and(self.mine >= 0, self.mine < self.owners)

    def rows(self, h, s):
        return pl.ds(pl.multiple_of(h * self.half + s * self.part, 8), self.part)

    def chunk_rows(self, h, s, j):
        return pl.ds(pl.multiple_of(h * self.half + s * self.part + j * self.chunk, 8), self.chunk)

    def far_owner(self, i):
        return lax.rem(i + jnp.where(self.low, self.owners // 2, 0), self.owners)

    def near_owner(self, i):
        return jnp.where(self.low, i, self.owners - 1 - i)

    def far_chip(self, i):
        return jnp.where(self.low, self.H - 1 - i, i)


class Reduce:
    def __init__(self, plan, mine, came, send, recv):
        self.p, self.mine, self.came, self.send, self.recv = plan, mine, came, send, recv

    def copy(self, j):
        p = self.p
        to = p.first + j
        slot = lax.rem(p.k - to + p.H, p.H) - 1
        return remote(self.mine.at[j], self.came.at[slot], self.send.at[j], self.recv.at[slot],
                      2 * to + p.h, p.g)

    def arrival(self, slot):
        p = self.p
        return remote(self.came.at[slot], self.came.at[slot], self.send.at[0], self.recv.at[slot],
                      p.partner, p.g)

    def start(self):
        p = self.p
        for i in range(p.owners):
            j = p.far_owner(i)
            pl.when(p.mine != j)(lambda: self.copy(j).start())

    def total(self):
        total = self.mine[self.p.mine]
        for slot in range(self.p.H - 1):
            self.arrival(slot).wait_recv()
            total = total + self.came[slot]
        return total

    def finish(self):
        p = self.p
        for i in range(p.owners):
            j = p.far_owner(i)
            pl.when(p.mine != j)(lambda: self.copy(j).wait_send())


class Gather:
    def __init__(self, plan, full, line, group, relay):
        self.p, self.full, self.line, self.group, self.relay = plan, full, line, group, relay

    def slot(self, h, s, j):
        return self.full.at[:, self.p.chunk_rows(h, s, j)]

    def line_copy(self, chip):
        p = self.p
        slot = self.slot(p.h, p.s, p.mine)
        return remote(slot, slot, self.line[0].at[chip], self.line[1].at[p.mine], 2 * chip + p.h, p.g)

    def line_arrival(self, j):
        p = self.p
        slot = self.slot(p.h, p.s, j)
        return remote(slot, slot, self.line[0].at[0], self.line[1].at[j], p.partner, p.g)

    def group_copy(self, d, j, arriving):
        p = self.p
        n = (d - 1) * p.owners + j
        s = lax.rem(p.s + (p.gs - d if arriving else d), p.gs)
        slot = self.slot(p.h, s if arriving else p.s, j)
        return remote(slot, slot, self.group[0].at[n], self.group[1].at[n], p.t, p.g - p.s + s)

    def relay_copy(self, d, j, arriving):
        p = self.p
        n = d * p.owners + j
        s = lax.rem(p.s + p.gs - d, p.gs)
        slot = self.slot(1 - p.h if arriving else p.h, s, j)
        return remote(slot, slot, self.relay[0].at[n], self.relay[1].at[n], p.partner, p.g)

    def hand_on(self, j):
        for d in range(1, self.p.gs):
            self.group_copy(d, j, False).start()
        self.relay_copy(0, j, False).start()

    def start(self):
        p = self.p
        self.hand_on(p.mine)
        for i in range(p.H):
            chip = p.far_chip(i)
            pl.when(p.k != chip)(lambda: self.line_copy(chip).start())

    def forward(self):
        p = self.p
        for i in range(p.owners):
            j = p.near_owner(i)

            @pl.when(p.mine != j)
            def _():
                self.line_arrival(j).wait_recv()
                self.hand_on(j)
        for i in range(p.owners):
            for d in range(1, p.gs):
                j = p.near_owner(i)
                self.group_copy(d, j, True).wait_recv()
                self.relay_copy(d, j, False).start()

    def finish(self):
        p = self.p
        for d in range(p.gs):
            for j in range(p.owners):
                self.relay_copy(d, j, True).wait_recv()

    def drain(self):
        p = self.p

        @pl.when(p.owner)
        def _():
            for chip in range(p.H):
                pl.when(p.k != chip)(lambda: self.line_copy(chip).wait_send())
        for j in range(p.owners):
            for d in range(1, p.gs):
                self.group_copy(d, j, False).wait_send()
            for d in range(p.gs):
                self.relay_copy(d, j, False).wait_send()


def body(T, G, row_in, column_in, live_in, obj, probe_in, amp, tables_in, new_obj, new_probe,
         scal_in, scal, probe, tables, load_sem, pad, amp_raw, amps, win, terms, light_terms, acc,
         acc_light, edge, edge_light, light_full, light_whole, light_pair, light_whole_pair,
         light_mine, light_came, grad, grad_pair, grad_mine, grad_came, reach, own_s, own_r, side_s,
         side_r, amp_s, amp_r, scal_s, scal_r, edge_s, edge_r, pair_s, pair_r, light_s, light_r,
         grad_s, grad_r, line_s, line_r, group_s, group_r, relay_s, relay_r):
    t, g = lax.axis_index("tile"), lax.axis_index("group")
    R, B = obj.shape[1:]
    W = probe.shape[1]
    rows = pad.shape[2]
    spare, blocks = rows - W, W // B
    p = Plan(T, G, W)
    p.here(t, g)
    not_first, not_last = t > 0, t < T - 1

    def span(group):
        return pl.ds(pl.multiple_of(group * R, 8), R)

    own = pad.at[1, :, span(g)]
    loads = [pltpu.make_async_copy(src, dst, load_sem.at[i]) for i, (src, dst) in enumerate(
        [(obj, own), (probe_in, probe), (tables_in, tables)]
        + [(amp.at[0, :, b * B:(b + 1) * B], amp_raw.at[b]) for b in range(blocks)])]
    for load in loads:
        load.start()

    barrier = pltpu.get_barrier_semaphore()
    count = G - 1
    for j in range(1, G):
        pl.semaphore_signal(barrier, inc=1, device_id={"tile": t, "group": lax.rem(g + j, G)},
                            device_id_type=MESH)
    for d in (-1, 1, -2, 2):
        there = jnp.logical_and(t + d >= 0, t + d < T)

        @pl.when(there)
        def _():
            pl.semaphore_signal(barrier, inc=1, device_id={"tile": t + d, "group": g},
                                device_id_type=MESH)
        count = count + there.astype(jnp.int32)
    line = lax.broadcasted_iota(jnp.int32, scal_in.shape, 0)
    scal_in[...] = jnp.where(line == 0, row_in[0], jnp.where(line == 1, column_in[0], live_in[0]))
    pl.semaphore_wait(barrier, count)

    def to_peer(j, ch, arriving):
        peer = lax.rem(g + (G - j if arriving else j), G)
        slot = pad.at[1, ch, span(peer if arriving else g)]
        n = 2 * (j - 1) + ch
        return remote(slot if arriving else obj.at[ch], slot, own_s.at[n], own_r.at[n], t, peer)

    def to_side(j, ch, right, arriving):
        who = lax.rem(g + G - j, G)
        dst = pad.at[0 if right else 2, ch, span(who)]
        src = pad.at[1, ch, span(who)] if j else obj.at[ch]
        n = 4 * j + 2 * ch + int(right)
        return remote(dst if arriving else src, dst, side_s.at[n], side_r.at[n],
                      (t + 1 if right else t - 1) if not arriving else (t - 1 if right else t + 1), g)

    def amp_copy(j, arriving):
        peer = lax.rem(g + (G - j if arriving else j), G)
        slot = amps.at[peer if arriving else g]
        return remote(slot, slot, amp_s.at[j - 1], amp_r.at[j - 1], t, peer)

    def scal_copy(j, arriving):
        peer = lax.rem(g + (G - j if arriving else j), G)
        slot = scal.at[peer if arriving else g]
        return remote(slot if arriving else scal_in, slot, scal_s.at[j - 1], scal_r.at[j - 1], t, peer)

    def edge_copy(src, dst, right, base, arriving):
        n = base + int(right)
        side = dst.at[0 if right else 1]
        if arriving:
            return remote(side, side, edge_s.at[n], edge_r.at[n], t - 1 if right else t + 1, g)
        return remote(src.at[2 if right else 0], side, edge_s.at[n], edge_r.at[n],
                      t + 1 if right else t - 1, g)

    def pair_copy(src, dst, n):
        return remote(src, dst, pair_s.at[n], pair_r.at[n], p.partner, g)

    def to_sides(j, ch):
        pl.when(not_first)(lambda: to_side(j, ch, False, False).start())
        pl.when(not_last)(lambda: to_side(j, ch, True, False).start())

    for ch in range(2):
        for j in range(1, G):
            to_peer(j, ch, False).start()
        to_sides(0, ch)
    for j in range(1, G):
        scal_copy(j, False).start()

    known, rounds = 1, []
    while known < p.H - 1:
        rounds.append(known)
        known *= 2

    def ends(d):
        return [(p.k - d, p.k >= d), (p.k + d, p.k + d < p.H)]

    def tell(i):
        for chip, there in ends(rounds[i]):
            @pl.when(there)
            def _():
                pl.semaphore_signal(reach.at[i], inc=1,
                                    device_id={"tile": 2 * chip + p.h, "group": g}, device_id_type=MESH)

    def hear(i):
        (_, below), (_, above) = ends(rounds[i])
        pl.semaphore_wait(reach.at[i], below.astype(jnp.int32) + above.astype(jnp.int32))

    tell(0)
    scal[g] = scal_in[...]

    for load in loads[3:]:
        load.wait()
    n = W // 2
    a = cat([cat([amp_raw[b, pl.ds(q, n, stride=2), :] for q in range(2)], 0) for b in range(blocks)], 1)
    at = lax.broadcasted_iota(jnp.int32, (W, W), 1)
    at = jnp.where(at < n, 2 * at, 2 * at - (W - 1))
    order = jnp.where(lax.broadcasted_iota(jnp.int32, (W, W), 0) == at, 1.0, 0.0).astype(BF16)
    top = a.astype(BF16)
    rest = a - top.astype(F32)
    middle, low = split(rest)
    amps[g] = mm(top, order) + (mm(middle, order) + mm(low, order))
    for j in range(1, G):
        amp_copy(j, False).start()

    @pl.when(t == 0)
    def _():
        pad[0] = jnp.zeros(pad.shape[1:], F32)
        edge[0] = jnp.zeros(edge.shape[1:], F32)
        edge_light[0] = jnp.zeros(edge_light.shape[1:], F32)

    @pl.when(t == T - 1)
    def _():
        pad[2] = jnp.zeros(pad.shape[1:], F32)
        edge[1] = jnp.zeros(edge.shape[1:], F32)
        edge_light[1] = jnp.zeros(edge_light.shape[1:], F32)

    terms[:, :, 0:spare] = jnp.zeros((2, blocks, spare, B), F32)
    terms[:, :, spare + W:] = jnp.zeros((2, blocks, spare, B), F32)
    light_terms[:, 0:spare] = jnp.zeros((blocks, spare, B), F32)
    light_terms[:, spare + W:] = jnp.zeros((blocks, spare, B), F32)

    def hold(ref, value):
        for b in range(blocks):
            ref[b, spare:spare + W] = value[:, b * B:(b + 1) * B]

    for load in loads[:3]:
        load.wait()
    probe_light = probe[0] * probe[0] + probe[1] * probe[1]
    hold(light_terms, probe_light)
    light_max = jnp.max(probe_light) + 1e-06

    for ch in range(2):
        for j in range(1, G):
            to_peer(j, ch, True).wait_recv()
            to_sides(j, ch)
    for i in range(len(rounds)):
        hear(i)
        if i + 1 < len(rounds):
            tell(i + 1)
    for j in range(1, G):
        scal_copy(j, True).wait_recv()
    for j in range(G):
        for ch in range(2):
            pl.when(not_last)(lambda: to_side(j, ch, False, True).wait_recv())
            pl.when(not_first)(lambda: to_side(j, ch, True, True).wait_recv())

    def numbers(k):
        return scal[k, 0, 0], scal[k, 1, 0], scal[k, 2, 0].astype(F32)

    def placed(ref, row, column):
        first = g * R + spare - row
        pieces = [ref[b, pl.ds(first, R), :] for b in range(blocks)]
        wide = cat(pieces + [jnp.zeros((R, 3 * B - W), F32)], 1)
        wide = pltpu.roll(wide, column, 1)
        return [wide[:, b * B:(b + 1) * B] for b in range(3)]

    def look(k, first):
        row, column, weight = numbers(k)
        for ch in range(2):
            wide = cat([pad[b, ch, pl.ds(row, W), :] for b in range(3)], 1)
            win[k, ch] = pltpu.roll(wide, lax.rem(3 * B - column, 3 * B), 1)[:, 0:W]
        for b, piece in enumerate(placed(light_terms, row, column)):
            piece = weight * piece
            acc_light[b] = piece if first else acc_light[b] + piece
        light = weight * (win[k, 0] * win[k, 0] + win[k, 1] * win[k, 1])
        light_full[...] = light if first else light_full[...] + light

    def position(k, first):
        row, column, weight = numbers(k)
        wr, wi = win[k, 0], win[k, 1]
        pr, pi = probe[0], probe[1]
        freq = fold_in(pr * wr - pi * wi, pr * wi + pi * wr, tables)
        scaled = []
        for q in range(2):
            fr, fi = freq[q][:, :n], freq[q][:, n:]
            factor = weight - (weight * amps[k, :, q * n:(q + 1) * n]) * lax.rsqrt(
                jnp.maximum(fr * fr + fi * fi, 0.0625))
            scaled.append(cat([fr * factor, fi * factor], 1))
        mr, mi = fold_out(*scaled, tables)
        pr, pi = probe[0], probe[1]
        wr, wi = win[k, 0], win[k, 1]
        for ch, value in enumerate((wr * mr + wi * mi, wr * mi - wi * mr)):
            grad[ch] = value if first else grad[ch] + value
        hold(terms.at[0], pr * mr + pi * mi)
        hold(terms.at[1], pr * mi - pi * mr)

    def add_terms(k, first):
        row, column, _ = numbers(k)
        for ch in range(2):
            for b, piece in enumerate(placed(terms.at[ch], row, column)):
                acc[b, ch] = piece if first else acc[b, ch] + piece

    def peers(f):
        if G == 2:
            f(1)
        elif G > 2:
            pl.loop(1, G)(f)

    look(g, True)
    peers(lambda j: look(lax.rem(g + G - j, G), False))
    light_whole[...] = jnp.sum(light_full[...].reshape(W // 8, 8, W), axis=0)
    light_pairs = [pair_copy(light_full.at[p.rows(1 - p.h, p.s)], light_pair, 0),
                   pair_copy(light_whole, light_whole_pair, 1)]
    for copy in light_pairs:
        copy.start()
    pl.when(not_first)(lambda: edge_copy(acc_light, edge_light, False, 0, False).start())
    pl.when(not_last)(lambda: edge_copy(acc_light, edge_light, True, 0, False).start())

    position(g, True)
    add_terms(g, True)

    for copy in light_pairs:
        copy.wait()
    whole = light_whole[...] + light_whole_pair[...]
    for j in range(p.owners):
        light_mine[j, 0:p.chunk] = (light_full[p.chunk_rows(p.h, p.s, j), :]
                                    + light_pair[j * p.chunk:(j + 1) * p.chunk, :])
        light_mine[j, p.chunk:] = whole
    light_red = Reduce(p, light_mine, light_came, light_s, light_r)
    light_red.start()

    def peer_position(j):
        amp_copy(j, True).wait_recv()
        k = lax.rem(g + G - j, G)
        position(k, False)
        if G > 2:
            add_terms(k, False)

    peers(peer_position)
    grad_pairs = pair_copy(grad.at[:, p.rows(1 - p.h, p.s)], grad_pair, 2)
    grad_pairs.start()
    if G == 2:
        add_terms(1 - g, False)
    grad_pairs.wait()
    for j in range(p.owners):
        grad_mine[j] = (grad[:, p.chunk_rows(p.h, p.s, j), :]
                        + grad_pair[:, j * p.chunk:(j + 1) * p.chunk, :])
    grad_red = Reduce(p, grad_mine, grad_came, grad_s, grad_r)
    grad_red.start()
    pl.when(not_first)(lambda: edge_copy(acc, edge, False, 2, False).start())
    pl.when(not_last)(lambda: edge_copy(acc, edge, True, 2, False).start())

    spread = Gather(p, new_probe, (line_s, line_r), (group_s, group_r), (relay_s, relay_r))

    @pl.when(p.owner)
    def _():
        light = light_red.total()
        mean = jnp.sum(light[p.chunk:]) * (1.0 / (W * W))
        below = 1.0 / (light[:p.chunk] + 0.25 * mean + 1e-05)
        here = p.chunk_rows(p.h, p.s, p.mine)
        total = grad_red.total()
        for ch in range(2):
            new_probe[ch, here, :] = probe[ch, here, :] - total[ch] * below
        spread.start()

    spread.forward()
    for src, dst, base in ((acc_light, edge_light, 0), (acc, edge, 2)):
        pl.when(not_last)(lambda: edge_copy(src, dst, False, base, True).wait_recv())
        pl.when(not_first)(lambda: edge_copy(src, dst, True, base, True).wait_recv())
    below = 1.0 / (acc_light[1] + edge_light[0] + edge_light[1] + 0.25 * light_max)
    for ch in range(2):
        new_obj[ch] = own[ch] - (acc[1, ch] + edge[0, ch] + edge[1, ch]) * below

    for j in range(1, G):
        for ch in range(2):
            to_peer(j, ch, False).wait_send()
        amp_copy(j, False).wait_send()
        scal_copy(j, False).wait_send()
    for j in range(G):
        for ch in range(2):
            pl.when(not_first)(lambda: to_side(j, ch, False, False).wait_send())
            pl.when(not_last)(lambda: to_side(j, ch, True, False).wait_send())
    for src, dst, base in ((acc_light, edge_light, 0), (acc, edge, 2)):
        pl.when(not_first)(lambda: edge_copy(src, dst, False, base, False).wait_send())
        pl.when(not_last)(lambda: edge_copy(src, dst, True, base, False).wait_send())
    light_red.finish()
    grad_red.finish()
    spread.finish()
    spread.drain()


def put(obj, probe, obj_out, probe_out, sems):
    copies = [pltpu.make_async_copy(obj, obj_out, sems.at[0]),
              pltpu.make_async_copy(probe, probe_out, sems.at[1])]
    for copy in copies:
        copy.start()
    for copy in copies:
        copy.wait()


def local(T, G, object_field, probe_field, amplitudes, row_start, column_start, live_slots):
    R, B = object_field.shape[1:]
    W = probe_field.shape[1]
    rows = R * G
    p = Plan(T, G, W)
    tables = dft_tables(W)
    spare, blocks = rows - W, W // B
    dma = lambda n: pltpu.SemaphoreType.DMA((max(n, 1),))
    vm = lambda *shape: pltpu.VMEM(shape, F32)

    vmem_limit = 67043328 - 4 * (object_field.size + probe_field.size) - 65536
    smem = pl.BlockSpec(memory_space=pltpu.SMEM)
    hbm = pl.BlockSpec(memory_space=pltpu.HBM)
    vmem = pl.BlockSpec(memory_space=pltpu.VMEM)
    new_obj, new_probe = pl.pallas_call(
        functools.partial(body, T, G),
        out_shape=(pltpu.VMEM(object_field.shape, F32), pltpu.VMEM(probe_field.shape, F32)),
        in_specs=[smem] * 3 + [hbm] * 4,
        out_specs=(vmem, vmem),
        scratch_shapes=[
            pltpu.VMEM((8, 128), jnp.int32),
            pltpu.VMEM((G, 8, 128), jnp.int32),
            vm(2, W, W),
            pltpu.VMEM(tables.shape, BF16),
            dma(3 + blocks),
            vm(3, 2, rows, B),
            vm(blocks, W, B), vm(G, W, W), vm(G, 2, W, W),
            vm(2, blocks, W + 2 * spare, B), vm(blocks, W + 2 * spare, B),
            vm(3, 2, R, B), vm(3, R, B), vm(2, 2, R, B), vm(2, R, B),
            vm(W, W), vm(8, W), vm(p.part, W), vm(8, W),
            vm(p.owners, p.chunk + 8, W), vm(p.H - 1, p.chunk + 8, W),
            vm(2, W, W), vm(2, p.part, W),
            vm(p.owners, 2, p.chunk, W), vm(p.H - 1, 2, p.chunk, W),
            pltpu.SemaphoreType.REGULAR((max(p.H.bit_length(), 1),)),
            dma(2 * G - 2), dma(2 * G - 2), dma(4 * G), dma(4 * G), dma(G - 1), dma(G - 1),
            dma(G - 1), dma(G - 1), dma(4), dma(4), dma(3), dma(3),
            dma(p.owners), dma(p.H - 1), dma(p.owners), dma(p.H - 1),
            dma(p.H), dma(p.owners), dma((p.gs - 1) * p.owners), dma((p.gs - 1) * p.owners),
            dma(p.gs * p.owners), dma(p.gs * p.owners),
        ],
        compiler_params=pltpu.CompilerParams(
            collective_id=0, has_side_effects=True, vmem_limit_bytes=vmem_limit),
    )(row_start, column_start, live_slots, object_field, probe_field, amplitudes, tables)
    anywhere = pl.BlockSpec(memory_space=pl.ANY)
    return pl.pallas_call(
        put,
        out_shape=(jax.ShapeDtypeStruct(object_field.shape, F32),
                   jax.ShapeDtypeStruct(probe_field.shape, F32)),
        in_specs=[vmem] * 2,
        out_specs=(anywhere, anywhere),
        scratch_shapes=[dma(2)],
        compiler_params=pltpu.CompilerParams(vmem_limit_bytes=1024 * 1024),
    )(new_obj, new_probe)


def solution(mesh):
    return jax.shard_map(
        functools.partial(local, mesh.shape["tile"], mesh.shape["group"]),
        mesh=mesh,
        in_specs=(
            P(None, "group", "tile"),
            P(),
            P(("tile", "group"), None, None),
            P(("tile", "group")),
            P(("tile", "group")),
            P(("tile", "group")),
        ),
        out_specs=(P(None, "group", "tile"), P()),
        check_vma=False,
    )
```

time: 45.2 us -> 38.7 us (0.86)
  Pallas kernels: 42.4 us -> 36 us
    pallas_call x1, Pallas kernels: 41.6 us -> 35.1 us  [local(): pl.pallas_call(functools.partial(body, T, G), out_shape=(pltpu.VMEM(objec...]
where the time goes in v1:
time: 38.7 us; the launch traced here: 38.6 us
  Pallas kernels  36 us (93%)
  between operations  2.58 us (7%)
    pallas_call x1, Pallas kernels, local(): pl.pallas_call(functools.partial(body, T, G), out_shape=(pltpu.VMEM(objec...  35.1 us
    pallas_call x1, Pallas kernels, local(): pl.pallas_call(put, out_shape=(jax.ShapeDtypeStruct(object_field.shape, F...  0.87 us

profile of v1, /device:TPU:0, one launch (start us, length us, event | category | flops | bytes accessed | tf_op | source)
XLA Modules:
  0.0 38.6 jit_solution(7761348869373992038)
XLA Ops:
  2.6 35.1 %shard_map.86 = (f32[2,160,128]{2,1,0:T(8,128)S(1)}, f32[2,256,256]{2,1,0:T(8,128)S(1)}) custom-call(s32[1]{0:T(128)S(6)} %copy.9.row_in, s32[1]{0:T(128)S(6)} %copy.10.column_in, s32[1]{0:T(128)S(6)} %copy.11.live_in, f32[2,160,128]{2,1,0:T(8,128)} %obj.1, f32[2,256,256]{2,1,0:T(8,128)} %probe_in.1, f32[1,256,256]{2,1,0:T(8,128)} %amp.1, ...), custom_call_target="tpu_custom_call" | custom-call | tf_op jit(solution)/shard_map/pallas_call | solution.py:568
  37.7 0.9 %shard_map.87 = (f32[2,160,128]{2,1,0:T(8,128)}, f32[2,256,256]{2,1,0:T(8,128)}) custom-call(f32[2,160,128]{2,1,0:T(8,128)S(1)} %get-tuple-element.4.obj, f32[2,256,256]{2,1,0:T(8,128)S(1)} %get-tuple-element.5.probe), custom_call_target="tpu_custom_call" | custom-call | tf_op jit(solution)/shard_map/pallas_call | solution.py:598

commit v2 on v1

--- a/solution.py
+++ b/solution.py
@@ -128,20 +128,18 @@
 
 
 class Reduce:
-    def __init__(self, plan, mine, came, send, recv):
-        self.p, self.mine, self.came, self.send, self.recv = plan, mine, came, send, recv
+    def __init__(self, plan, mine, came, sems):
+        self.p, self.mine, self.came, self.sems = plan, mine, came, sems
 
     def copy(self, j):
         p = self.p
         to = p.first + j
         slot = lax.rem(p.k - to + p.H, p.H) - 1
-        return remote(self.mine.at[j], self.came.at[slot], self.send.at[j], self.recv.at[slot],
+        return remote(self.mine.at[j], self.came.at[slot], self.sems.at[0], self.sems.at[1],
                       2 * to + p.h, p.g)
 
-    def arrival(self, slot):
-        p = self.p
-        return remote(self.came.at[slot], self.came.at[slot], self.send.at[0], self.recv.at[slot],
-                      p.partner, p.g)
+    def bytes_of(self, ref):
+        return remote(ref, ref, self.sems.at[0], self.sems.at[1], self.p.partner, self.p.g)
 
     def start(self):
         p = self.p
@@ -150,54 +148,55 @@
             pl.when(p.mine != j)(lambda: self.copy(j).start())
 
     def total(self):
+        self.bytes_of(self.came).wait_recv()
         total = self.mine[self.p.mine]
         for slot in range(self.p.H - 1):
-            self.arrival(slot).wait_recv()
             total = total + self.came[slot]
         return total
 
     def finish(self):
         p = self.p
-        for i in range(p.owners):
-            j = p.far_owner(i)
-            pl.when(p.mine != j)(lambda: self.copy(j).wait_send())
+        pl.when(p.owner)(lambda: self.bytes_of(self.mine.at[0:p.owners - 1]).wait_send())
+        pl.when(jnp.logical_not(p.owner))(lambda: self.bytes_of(self.mine).wait_send())
 
 
 class Gather:
-    def __init__(self, plan, full, line, group, relay):
-        self.p, self.full, self.line, self.group, self.relay = plan, full, line, group, relay
+    def __init__(self, plan, full, spare, sent, line, group, relay):
+        self.p, self.full, self.spare, self.sent = plan, full, spare, sent
+        self.line, self.group, self.relay = line, group, relay
 
     def slot(self, h, s, j):
-        return self.full.at[:, self.p.chunk_rows(h, s, j)]
+        return self.full.at[h, s, j]
 
     def line_copy(self, chip):
         p = self.p
         slot = self.slot(p.h, p.s, p.mine)
-        return remote(slot, slot, self.line[0].at[chip], self.line[1].at[p.mine], 2 * chip + p.h, p.g)
+        return remote(slot, slot, self.sent.at[0], self.line.at[p.mine], 2 * chip + p.h, p.g)
 
     def line_arrival(self, j):
         p = self.p
         slot = self.slot(p.h, p.s, j)
-        return remote(slot, slot, self.line[0].at[0], self.line[1].at[j], p.partner, p.g)
+        return remote(slot, slot, self.sent.at[0], self.line.at[j], p.partner, p.g)
 
     def group_copy(self, d, j, arriving):
         p = self.p
         n = (d - 1) * p.owners + j
         s = lax.rem(p.s + (p.gs - d if arriving else d), p.gs)
         slot = self.slot(p.h, s if arriving else p.s, j)
-        return remote(slot, slot, self.group[0].at[n], self.group[1].at[n], p.t, p.g - p.s + s)
-
-    def relay_copy(self, d, j, arriving):
-        p = self.p
-        n = d * p.owners + j
-        s = lax.rem(p.s + p.gs - d, p.gs)
-        slot = self.slot(1 - p.h if arriving else p.h, s, j)
-        return remote(slot, slot, self.relay[0].at[n], self.relay[1].at[n], p.partner, p.g)
+        return remote(slot, slot, self.sent.at[1], self.group.at[n], p.t, p.g - p.s + s)
+
+    def relay_copy(self, d, j):
+        p = self.p
+        slot = self.slot(p.h, lax.rem(p.s + p.gs - d, p.gs), j)
+        return remote(slot, slot, self.sent.at[2], self.relay.at[0], p.partner, p.g)
+
+    def bytes_of(self, ref, n):
+        return remote(ref, ref, self.sent.at[n], self.relay.at[0], self.p.partner, self.p.g)
 
     def hand_on(self, j):
         for d in range(1, self.p.gs):
             self.group_copy(d, j, False).start()
-        self.relay_copy(0, j, False).start()
+        self.relay_copy(0, j).start()
 
     def start(self):
         p = self.p
@@ -219,34 +218,25 @@
             for d in range(1, p.gs):
                 j = p.near_owner(i)
                 self.group_copy(d, j, True).wait_recv()
-                self.relay_copy(d, j, False).start()
+                self.relay_copy(d, j).start()
 
     def finish(self):
-        p = self.p
-        for d in range(p.gs):
-            for j in range(p.owners):
-                self.relay_copy(d, j, True).wait_recv()
+        self.bytes_of(self.full.at[1 - self.p.h], 2).wait_recv()
 
     def drain(self):
         p = self.p
-
-        @pl.when(p.owner)
-        def _():
-            for chip in range(p.H):
-                pl.when(p.k != chip)(lambda: self.line_copy(chip).wait_send())
-        for j in range(p.owners):
-            for d in range(1, p.gs):
-                self.group_copy(d, j, False).wait_send()
-            for d in range(p.gs):
-                self.relay_copy(d, j, False).wait_send()
+        pl.when(p.owner)(lambda: self.bytes_of(self.spare, 0).wait_send())
+        if p.gs > 1:
+            self.bytes_of(self.full.at[0, 0:p.gs - 1], 1).wait_send()
+        self.bytes_of(self.full.at[0], 2).wait_send()
 
 
 def body(T, G, row_in, column_in, live_in, obj, probe_in, amp, tables_in, new_obj, new_probe,
          scal_in, scal, probe, tables, load_sem, pad, amp_raw, amps, win, terms, light_terms, acc,
-         acc_light, edge, edge_light, light_full, light_whole, light_pair, light_whole_pair,
-         light_mine, light_came, grad, grad_pair, grad_mine, grad_came, reach, own_s, own_r, side_s,
-         side_r, amp_s, amp_r, scal_s, scal_r, edge_s, edge_r, pair_s, pair_r, light_s, light_r,
-         grad_s, grad_r, line_s, line_r, group_s, group_r, relay_s, relay_r):
+         acc_light, edge, edge_light, light_full, light_whole, light_pair, light_mine, light_came,
+         grad, grad_pair, grad_mine, grad_came, full, reach, own_s, own_r, side_s, side_r, amp_s,
+         amp_r, scal_s, edge_s, edge_r, pair_s, pair_r, light_s, grad_s, sent, line_r, group_r,
+         relay_r):
     t, g = lax.axis_index("tile"), lax.axis_index("group")
     R, B = obj.shape[1:]
     W = probe.shape[1]
@@ -261,9 +251,10 @@
 
     own = pad.at[1, :, span(g)]
     loads = [pltpu.make_async_copy(src, dst, load_sem.at[i]) for i, (src, dst) in enumerate(
-        [(obj, own), (probe_in, probe), (tables_in, tables)]
-        + [(amp.at[0, :, b * B:(b + 1) * B], amp_raw.at[b]) for b in range(blocks)])]
-    for load in loads:
+        [(obj, own), (probe_in, probe), (tables_in, tables)])]
+    amp_loads = [pltpu.make_async_copy(amp.at[0, :, b * B:(b + 1) * B], amp_raw.at[b], load_sem.at[3])
+                 for b in range(blocks)]
+    for load in amp_loads + loads:
         load.start()
 
     barrier = pltpu.get_barrier_semaphore()
@@ -283,51 +274,64 @@
     scal_in[...] = jnp.where(line == 0, row_in[0], jnp.where(line == 1, column_in[0], live_in[0]))
     pl.semaphore_wait(barrier, count)
 
-    def to_peer(j, ch, arriving):
+    cut_row = R // 16 * 8
+    pieces = [(0, cut_row), (cut_row, R - cut_row)] if cut_row else [(0, R)]
+
+    def piece(group, q):
+        return pl.ds(pl.multiple_of(group * R + pieces[q][0], 8), pieces[q][1])
+
+    def to_peer(j, ch, q, arriving):
         peer = lax.rem(g + (G - j if arriving else j), G)
-        slot = pad.at[1, ch, span(peer if arriving else g)]
-        n = 2 * (j - 1) + ch
-        return remote(slot if arriving else obj.at[ch], slot, own_s.at[n], own_r.at[n], t, peer)
-
-    def to_side(j, ch, right, arriving):
-        who = lax.rem(g + G - j, G)
-        dst = pad.at[0 if right else 2, ch, span(who)]
-        src = pad.at[1, ch, span(who)] if j else obj.at[ch]
-        n = 4 * j + 2 * ch + int(right)
-        return remote(dst if arriving else src, dst, side_s.at[n], side_r.at[n],
-                      (t + 1 if right else t - 1) if not arriving else (t - 1 if right else t + 1), g)
+        slot = pad.at[1, ch, piece(peer if arriving else g, q)]
+        n = (2 * (j - 1) + ch) * len(pieces) + q
+        src = slot if arriving else obj.at[ch, pieces[q][0]:pieces[q][0] + pieces[q][1]]
+        return remote(src, slot, own_s.at[0], own_r.at[n], t, peer)
+
+    def to_side(ch, right, src, rows_of):
+        dst = pad.at[0 if right else 2, ch, rows_of]
+        return remote(src, dst, side_s.at[int(right)], side_r.at[2 * ch + int(right)],
+                      t + 1 if right else t - 1, g)
+
+    def side_bytes(ref, ch, right):
+        return remote(ref, ref, side_s.at[int(right)], side_r.at[2 * ch + int(right)], p.partner, g)
 
     def amp_copy(j, arriving):
         peer = lax.rem(g + (G - j if arriving else j), G)
         slot = amps.at[peer if arriving else g]
-        return remote(slot, slot, amp_s.at[j - 1], amp_r.at[j - 1], t, peer)
-
-    def scal_copy(j, arriving):
-        peer = lax.rem(g + (G - j if arriving else j), G)
-        slot = scal.at[peer if arriving else g]
-        return remote(slot if arriving else scal_in, slot, scal_s.at[j - 1], scal_r.at[j - 1], t, peer)
+        return remote(slot, slot, amp_s.at[0], amp_r.at[j - 1], t, peer)
+
+    def scal_copy(j):
+        return remote(scal_in, scal.at[g], scal_s.at[0], scal_s.at[1], t, lax.rem(g + j, G))
+
+    def bytes_of(ref, send, recv):
+        return remote(ref, ref, send, recv, p.partner, g)
 
     def edge_copy(src, dst, right, base, arriving):
         n = base + int(right)
         side = dst.at[0 if right else 1]
         if arriving:
-            return remote(side, side, edge_s.at[n], edge_r.at[n], t - 1 if right else t + 1, g)
-        return remote(src.at[2 if right else 0], side, edge_s.at[n], edge_r.at[n],
+            return remote(side, side, edge_s.at[int(right)], edge_r.at[n], t - 1 if right else t + 1, g)
+        return remote(src.at[2 if right else 0], side, edge_s.at[int(right)], edge_r.at[n],
                       t + 1 if right else t - 1, g)
+
+    def edges_sent(src, dst, base):
+        pl.when(not_first)(lambda: edge_copy(src, dst, False, base, False).wait_send())
+        pl.when(not_last)(lambda: edge_copy(src, dst, True, base, False).wait_send())
 
     def pair_copy(src, dst, n):
         return remote(src, dst, pair_s.at[n], pair_r.at[n], p.partner, g)
 
-    def to_sides(j, ch):
-        pl.when(not_first)(lambda: to_side(j, ch, False, False).start())
-        pl.when(not_last)(lambda: to_side(j, ch, True, False).start())
+    def to_sides(ch, src, rows_of):
+        pl.when(not_first)(lambda: to_side(ch, False, src, rows_of).start())
+        pl.when(not_last)(lambda: to_side(ch, True, src, rows_of).start())
 
     for ch in range(2):
-        for j in range(1, G):
-            to_peer(j, ch, False).start()
-        to_sides(0, ch)
+        for q in range(len(pieces)):
+            for j in range(1, G):
+                to_peer(j, ch, q, False).start()
+        to_sides(ch, obj.at[ch], span(g))
     for j in range(1, G):
-        scal_copy(j, False).start()
+        scal_copy(j).start()
 
     known, rounds = 1, []
     while known < p.H - 1:
@@ -351,8 +355,7 @@
     tell(0)
     scal[g] = scal_in[...]
 
-    for load in loads[3:]:
-        load.wait()
+    pltpu.make_async_copy(amp_raw, amp_raw, load_sem.at[3]).wait()
     n = W // 2
     a = cat([cat([amp_raw[b, pl.ds(q, n, stride=2), :] for q in range(2)], 0) for b in range(blocks)], 1)
     at = lax.broadcasted_iota(jnp.int32, (W, W), 1)
@@ -386,45 +389,56 @@
         for b in range(blocks):
             ref[b, spare:spare + W] = value[:, b * B:(b + 1) * B]
 
-    for load in loads[:3]:
+    for load in loads:
         load.wait()
     probe_light = probe[0] * probe[0] + probe[1] * probe[1]
     hold(light_terms, probe_light)
     light_max = jnp.max(probe_light) + 1e-06
 
     for ch in range(2):
-        for j in range(1, G):
-            to_peer(j, ch, True).wait_recv()
-            to_sides(j, ch)
-    for i in range(len(rounds)):
+        for q in range(len(pieces)):
+            for j in range(1, G):
+                to_peer(j, ch, q, True).wait_recv()
+                rows_of = piece(lax.rem(g + G - j, G), q)
+                to_sides(ch, pad.at[1, ch, rows_of], rows_of)
+    if G > 1:
+        bytes_of(scal.at[0:G - 1], scal_s.at[0], scal_s.at[1]).wait_recv()
+
+    def next_round(i):
         hear(i)
         if i + 1 < len(rounds):
             tell(i + 1)
-    for j in range(1, G):
-        scal_copy(j, True).wait_recv()
-    for j in range(G):
-        for ch in range(2):
-            pl.when(not_last)(lambda: to_side(j, ch, False, True).wait_recv())
-            pl.when(not_first)(lambda: to_side(j, ch, True, True).wait_recv())
 
     def numbers(k):
         return scal[k, 0, 0], scal[k, 1, 0], scal[k, 2, 0].astype(F32)
 
+    lane = lax.broadcasted_iota(jnp.int32, (8, B), 1)[0:1]
+
     def placed(ref, row, column):
         first = g * R + spare - row
-        pieces = [ref[b, pl.ds(first, R), :] for b in range(blocks)]
-        wide = cat(pieces + [jnp.zeros((R, 3 * B - W), F32)], 1)
-        wide = pltpu.roll(wide, column, 1)
-        return [wide[:, b * B:(b + 1) * B] for b in range(3)]
-
-    def look(k, first):
+        shift = lax.rem(column, B)
+        stay = lane >= column
+        pieces = [pltpu.roll(ref[b, pl.ds(first, R), :], shift, 1) for b in range(blocks)]
+        out = [jnp.where(stay, pieces[0], 0.0)]
+        out += [jnp.where(stay, pieces[b], pieces[b - 1]) for b in range(1, blocks)]
+        return out + [jnp.where(stay, 0.0, pieces[-1])]
+
+    def cut(k, ch):
+        row, column, _ = numbers(k)
+        shift = lax.rem(B - lax.rem(column, B), B)
+        stay = lane < B - column
+        pieces = [pltpu.roll(pad[b, ch, pl.ds(row, W), :], shift, 1) for b in range(blocks + 1)]
+        for b in range(blocks):
+            win[k, ch, :, b * B:(b + 1) * B] = jnp.where(stay, pieces[b], pieces[b + 1])
+
+    def place_light(k, first):
         row, column, weight = numbers(k)
-        for ch in range(2):
-            wide = cat([pad[b, ch, pl.ds(row, W), :] for b in range(3)], 1)
-            win[k, ch] = pltpu.roll(wide, lax.rem(3 * B - column, 3 * B), 1)[:, 0:W]
         for b, piece in enumerate(placed(light_terms, row, column)):
             piece = weight * piece
             acc_light[b] = piece if first else acc_light[b] + piece
+
+    def look(k, first):
+        weight = numbers(k)[2]
         light = weight * (win[k, 0] * win[k, 0] + win[k, 1] * win[k, 1])
         light_full[...] = light if first else light_full[...] + light
 
@@ -459,27 +473,37 @@
         elif G > 2:
             pl.loop(1, G)(f)
 
+    place_light(g, True)
+    peers(lambda j: place_light(lax.rem(g + G - j, G), False))
+    next_round(0)
+    for ch in range(2):
+        pl.when(not_last)(lambda: side_bytes(pad.at[2, ch], ch, False).wait_recv())
+        pl.when(not_first)(lambda: side_bytes(pad.at[0, ch], ch, True).wait_recv())
+    for ch in range(2):
+        cut(g, ch)
+        peers(lambda j: cut(lax.rem(g + G - j, G), ch))
     look(g, True)
     peers(lambda j: look(lax.rem(g + G - j, G), False))
     light_whole[...] = jnp.sum(light_full[...].reshape(W // 8, 8, W), axis=0)
-    light_pairs = [pair_copy(light_full.at[p.rows(1 - p.h, p.s)], light_pair, 0),
-                   pair_copy(light_whole, light_whole_pair, 1)]
-    for copy in light_pairs:
-        copy.start()
+    pair_copy(light_full.at[p.rows(1 - p.h, p.s)], light_pair.at[0:p.part], 0).start()
+    pair_copy(light_whole, light_pair.at[p.part:p.part + 8], 0).start()
     pl.when(not_first)(lambda: edge_copy(acc_light, edge_light, False, 0, False).start())
     pl.when(not_last)(lambda: edge_copy(acc_light, edge_light, True, 0, False).start())
+    if len(rounds) > 1:
+        next_round(1)
 
     position(g, True)
     add_terms(g, True)
 
-    for copy in light_pairs:
-        copy.wait()
-    whole = light_whole[...] + light_whole_pair[...]
+    for i in range(2, len(rounds)):
+        next_round(i)
+    pair_copy(light_pair, light_pair, 0).wait()
+    whole = light_whole[...] + light_pair[p.part:, :]
     for j in range(p.owners):
         light_mine[j, 0:p.chunk] = (light_full[p.chunk_rows(p.h, p.s, j), :]
                                     + light_pair[j * p.chunk:(j + 1) * p.chunk, :])
         light_mine[j, p.chunk:] = whole
-    light_red = Reduce(p, light_mine, light_came, light_s, light_r)
+    light_red = Reduce(p, light_mine, light_came, light_s)
     light_red.start()
 
     def peer_position(j):
@@ -490,7 +514,7 @@
             add_terms(k, False)
 
     peers(peer_position)
-    grad_pairs = pair_copy(grad.at[:, p.rows(1 - p.h, p.s)], grad_pair, 2)
+    grad_pairs = pair_copy(grad.at[:, p.rows(1 - p.h, p.s)], grad_pair, 1)
     grad_pairs.start()
     if G == 2:
         add_terms(1 - g, False)
@@ -498,12 +522,13 @@
     for j in range(p.owners):
         grad_mine[j] = (grad[:, p.chunk_rows(p.h, p.s, j), :]
                         + grad_pair[:, j * p.chunk:(j + 1) * p.chunk, :])
-    grad_red = Reduce(p, grad_mine, grad_came, grad_s, grad_r)
+    grad_red = Reduce(p, grad_mine, grad_came, grad_s)
     grad_red.start()
+    edges_sent(acc_light, edge_light, 0)
     pl.when(not_first)(lambda: edge_copy(acc, edge, False, 2, False).start())
     pl.when(not_last)(lambda: edge_copy(acc, edge, True, 2, False).start())
 
-    spread = Gather(p, new_probe, (line_s, line_r), (group_s, group_r), (relay_s, relay_r))
+    spread = Gather(p, full, grad_came, sent, line_r, group_r, relay_r)
 
     @pl.when(p.owner)
     def _():
@@ -513,7 +538,7 @@
         here = p.chunk_rows(p.h, p.s, p.mine)
         total = grad_red.total()
         for ch in range(2):
-            new_probe[ch, here, :] = probe[ch, here, :] - total[ch] * below
+            full[p.h, p.s, p.mine, ch] = probe[ch, here, :] - total[ch] * below
         spread.start()
 
     spread.forward()
@@ -524,21 +549,18 @@
     for ch in range(2):
         new_obj[ch] = own[ch] - (acc[1, ch] + edge[0, ch] + edge[1, ch]) * below
 
-    for j in range(1, G):
-        for ch in range(2):
-            to_peer(j, ch, False).wait_send()
-        amp_copy(j, False).wait_send()
-        scal_copy(j, False).wait_send()
-    for j in range(G):
-        for ch in range(2):
-            pl.when(not_first)(lambda: to_side(j, ch, False, False).wait_send())
-            pl.when(not_last)(lambda: to_side(j, ch, True, False).wait_send())
-    for src, dst, base in ((acc_light, edge_light, 0), (acc, edge, 2)):
-        pl.when(not_first)(lambda: edge_copy(src, dst, False, base, False).wait_send())
-        pl.when(not_last)(lambda: edge_copy(src, dst, True, base, False).wait_send())
+    if G > 1:
+        bytes_of(pad.at[1, :, 0:(G - 1) * R], own_s.at[0], own_s.at[0]).wait_send()
+        bytes_of(amps.at[0:G - 1], amp_s.at[0], amp_s.at[0]).wait_send()
+        bytes_of(scal.at[0:G - 1], scal_s.at[0], scal_s.at[1]).wait_send()
+    pl.when(not_first)(lambda: side_bytes(pad.at[0], 0, False).wait_send())
+    pl.when(not_last)(lambda: side_bytes(pad.at[0], 0, True).wait_send())
+    edges_sent(acc, edge, 2)
     light_red.finish()
     grad_red.finish()
     spread.finish()
+    for ch in range(2):
+        new_probe[ch] = full[:, :, :, ch].reshape(W, W)
     spread.drain()
 
 
@@ -575,21 +597,19 @@
             pltpu.VMEM((G, 8, 128), jnp.int32),
             vm(2, W, W),
             pltpu.VMEM(tables.shape, BF16),
-            dma(3 + blocks),
+            dma(4),
             vm(3, 2, rows, B),
             vm(blocks, W, B), vm(G, W, W), vm(G, 2, W, W),
             vm(2, blocks, W + 2 * spare, B), vm(blocks, W + 2 * spare, B),
             vm(3, 2, R, B), vm(3, R, B), vm(2, 2, R, B), vm(2, R, B),
-            vm(W, W), vm(8, W), vm(p.part, W), vm(8, W),
+            vm(W, W), vm(8, W), vm(p.part + 8, W),
             vm(p.owners, p.chunk + 8, W), vm(p.H - 1, p.chunk + 8, W),
             vm(2, W, W), vm(2, p.part, W),
             vm(p.owners, 2, p.chunk, W), vm(p.H - 1, 2, p.chunk, W),
-            pltpu.SemaphoreType.REGULAR((max(p.H.bit_length(), 1),)),
-            dma(2 * G - 2), dma(2 * G - 2), dma(4 * G), dma(4 * G), dma(G - 1), dma(G - 1),
-            dma(G - 1), dma(G - 1), dma(4), dma(4), dma(3), dma(3),
-            dma(p.owners), dma(p.H - 1), dma(p.owners), dma(p.H - 1),
-            dma(p.H), dma(p.owners), dma((p.gs - 1) * p.owners), dma((p.gs - 1) * p.owners),
-            dma(p.gs * p.owners), dma(p.gs * p.owners),
+            vm(2, p.gs, p.owners, 2, p.chunk, W),
+            pltpu.SemaphoreType.REGULAR((max((p.H - 2).bit_length(), 1),)),
+            dma(1), dma(4 * G - 4), dma(2), dma(4), dma(1), dma(G - 1), dma(2), dma(2), dma(4),
+            dma(2), dma(2), dma(2), dma(2), dma(3), dma(p.owners), dma((p.gs - 1) * p.owners), dma(1),
         ],
         compiler_params=pltpu.CompilerParams(
             collective_id=0, has_side_effects=True, vmem_limit_bytes=vmem_limit),

time: 38.7 us -> 37.6 us (0.972)
  Pallas kernels: 36 us -> 34.9 us
    pallas_call x1, Pallas kernels: 35.1 us -> 34 us  [local(): pl.pallas_call(functools.partial(body, T, G), out_shape=(pltpu.VMEM(objec...]
where the time goes in v2:
time: 37.6 us; the launch traced here: 37.5 us
  Pallas kernels  34.9 us (93%)
  between operations  2.58 us (7%)
    pallas_call x1, Pallas kernels, local(): pl.pallas_call(functools.partial(body, T, G), out_shape=(pltpu.VMEM(objec...  34 us
    pallas_call x1, Pallas kernels, local(): pl.pallas_call(put, out_shape=(jax.ShapeDtypeStruct(object_field.shape, F...  0.87 us

profile of v2, /device:TPU:0, one launch (start us, length us, event | category | flops | bytes accessed | tf_op | source)
XLA Modules:
  0.0 37.5 jit_solution(16404534611655656257)
XLA Ops:
  2.6 34.0 %shard_map.86 = (f32[2,160,128]{2,1,0:T(8,128)S(1)}, f32[2,256,256]{2,1,0:T(8,128)S(1)}) custom-call(s32[1]{0:T(128)S(6)} %copy.9.row_in, s32[1]{0:T(128)S(6)} %copy.10.column_in, s32[1]{0:T(128)S(6)} %copy.11.live_in, f32[2,160,128]{2,1,0:T(8,128)} %obj.1, f32[2,256,256]{2,1,0:T(8,128)} %probe_in.1, f32[1,256,256]{2,1,0:T(8,128)} %amp.1, ...), custom_call_target="tpu_custom_call" | custom-call | tf_op jit(solution)/shard_map/pallas_call | solution.py:590
  36.6 0.9 %shard_map.87 = (f32[2,160,128]{2,1,0:T(8,128)}, f32[2,256,256]{2,1,0:T(8,128)}) custom-call(f32[2,160,128]{2,1,0:T(8,128)S(1)} %get-tuple-element.4.obj, f32[2,256,256]{2,1,0:T(8,128)S(1)} %get-tuple-element.5.probe), custom_call_target="tpu_custom_call" | custom-call | tf_op jit(solution)/shard_map/pallas_call | solution.py:618

commit v3 on v2

--- a/solution.py
+++ b/solution.py
@@ -56,33 +56,39 @@
     return mm(cat([head, tail, head], 1), cat([table[0], table[0], table[1]], 0))
 
 
-def fold_in(xr, xi, tables):
-    n = xr.shape[0] // 2
-    a = cat([xr[:n] + xr[n:], xi[:n] + xi[n:]], 0)
-    b = cat([xr[:n] - xr[n:], xi[:n] - xi[n:]], 0)
-    halves = table_left(tables[EVEN], a), table_left(tables[ODD], b)
+def fold_in(exits, tables):
+    n = exits[0][0].shape[0] // 2
+    halves = []
+    for sign, table in ((1, tables[EVEN]), (-1, tables[ODD])):
+        halves.append(table_left(table, cat(
+            [cat([x[:n] + sign * x[n:] for x in parts], 0) for parts in exits], 1)))
 
     def sides(sign):
         rows = []
-        for y in halves:
-            yr, yi = y[:n], y[n:]
-            rows.append(cat([yr[:, :n] + sign * yr[:, n:], yi[:, :n] + sign * yi[:, n:]], 1))
+        for i in range(len(exits)):
+            for y in halves:
+                y = y[:, 2 * n * i:2 * n * (i + 1)]
+                rows.append(cat([part[:, :n] + sign * part[:, n:] for part in (y[:n], y[n:])], 1))
         return cat(rows, 0)
 
     return table_right(sides(1), tables[EVEN_T]), table_right(sides(-1), tables[ODD_T])
 
 
 def fold_out(even, odd, tables):
-    n = even.shape[0] // 2
+    n = even.shape[1] // 2
     e, o = table_right(even, tables[EVEN]), table_right(odd, tables[ODD])
     plus, minus = e + o, e - o
+    count = even.shape[0] // (2 * n)
     halves = []
     for q, table in ((0, tables[EVEN_T]), (1, tables[ODD_T])):
-        r = slice(q * n, (q + 1) * n)
-        halves.append(table_left(table, cat(
-            [cat([plus[r, :n], minus[r, :n]], 1), cat([plus[r, n:], minus[r, n:]], 1)], 0)))
+        parts = []
+        for i in range(count):
+            r = slice((2 * i + q) * n, (2 * i + q + 1) * n)
+            parts.append(cat([cat([plus[r, :n], minus[r, :n]], 1), cat([plus[r, n:], minus[r, n:]], 1)], 0))
+        halves.append(table_left(table, cat(parts, 1)))
     plus, minus = halves[0] + halves[1], halves[0] - halves[1]
-    return cat([plus[:n], minus[:n]], 0), cat([plus[n:], minus[n:]], 0)
+    return [tuple(cat([side[part, 2 * n * i:2 * n * (i + 1)] for side in (plus, minus)], 0)
+                  for part in (slice(0, n), slice(n, 2 * n))) for i in range(count)]
 
 
 def remote(src, dst, send, recv, tile, group):
@@ -232,7 +238,7 @@
 
 
 def body(T, G, row_in, column_in, live_in, obj, probe_in, amp, tables_in, new_obj, new_probe,
-         scal_in, scal, probe, tables, load_sem, pad, amp_raw, amps, win, terms, light_terms, acc,
+         scal_in, scal, probe, tables, load_sem, pad, amp_raw, amps, win, freq, terms, light_terms, acc,
          acc_light, edge, edge_light, light_full, light_whole, light_pair, light_mine, light_came,
          grad, grad_pair, grad_mine, grad_came, full, reach, own_s, own_r, side_s, side_r, amp_s,
          amp_r, scal_s, edge_s, edge_r, pair_s, pair_r, light_s, grad_s, sent, line_r, group_r,
@@ -380,8 +386,8 @@
         edge[1] = jnp.zeros(edge.shape[1:], F32)
         edge_light[1] = jnp.zeros(edge_light.shape[1:], F32)
 
-    terms[:, :, 0:spare] = jnp.zeros((2, blocks, spare, B), F32)
-    terms[:, :, spare + W:] = jnp.zeros((2, blocks, spare, B), F32)
+    terms[:, :, :, 0:spare] = jnp.zeros((2, 2, blocks, spare, B), F32)
+    terms[:, :, :, spare + W:] = jnp.zeros((2, 2, blocks, spare, B), F32)
     light_terms[:, 0:spare] = jnp.zeros((blocks, spare, B), F32)
     light_terms[:, spare + W:] = jnp.zeros((blocks, spare, B), F32)
 
@@ -442,29 +448,43 @@
         light = weight * (win[k, 0] * win[k, 0] + win[k, 1] * win[k, 1])
         light_full[...] = light if first else light_full[...] + light
 
-    def position(k, first):
-        row, column, weight = numbers(k)
-        wr, wi = win[k, 0], win[k, 1]
+    def ahead(ks):
         pr, pi = probe[0], probe[1]
-        freq = fold_in(pr * wr - pi * wi, pr * wi + pi * wr, tables)
+        exits = []
+        for k in ks:
+            wr, wi = win[k, 0], win[k, 1]
+            exits.append((pr * wr - pi * wi, pr * wi + pi * wr))
+        for q, value in enumerate(fold_in(exits, tables)):
+            freq[q, 0:len(ks) * W] = value
+
+    def behind(ks, first):
         scaled = []
         for q in range(2):
-            fr, fi = freq[q][:, :n], freq[q][:, n:]
-            factor = weight - (weight * amps[k, :, q * n:(q + 1) * n]) * lax.rsqrt(
-                jnp.maximum(fr * fr + fi * fi, 0.0625))
-            scaled.append(cat([fr * factor, fi * factor], 1))
-        mr, mi = fold_out(*scaled, tables)
-        pr, pi = probe[0], probe[1]
-        wr, wi = win[k, 0], win[k, 1]
-        for ch, value in enumerate((wr * mr + wi * mi, wr * mi - wi * mr)):
-            grad[ch] = value if first else grad[ch] + value
-        hold(terms.at[0], pr * mr + pi * mi)
-        hold(terms.at[1], pr * mi - pi * mr)
-
-    def add_terms(k, first):
-        row, column, _ = numbers(k)
+            rows = []
+            for i, k in enumerate(ks):
+                value = freq[q, i * W:(i + 1) * W]
+                fr, fi = value[:, :n], value[:, n:]
+                weight = numbers(k)[2]
+                factor = weight - (weight * amps[k, :, q * n:(q + 1) * n]) * lax.rsqrt(
+                    jnp.maximum(fr * fr + fi * fi, 0.0625))
+                rows.append(cat([fr * factor, fi * factor], 1))
+            scaled.append(cat(rows, 0))
+        total = None
+        for i, (k, (mr, mi)) in enumerate(zip(ks, fold_out(*scaled, tables))):
+            wr, wi = win[k, 0], win[k, 1]
+            pr, pi = probe[0], probe[1]
+            both = (wr * mr + wi * mi, wr * mi - wi * mr)
+            total = both if total is None else [a + b for a, b in zip(total, both)]
+            hold(terms.at[i, 0], pr * mr + pi * mi)
+            hold(terms.at[i, 1], pr * mi - pi * mr)
         for ch in range(2):
-            for b, piece in enumerate(placed(terms.at[ch], row, column)):
+            grad[ch] = total[ch] if first else grad[ch] + total[ch]
+
+    def add_terms(ks, first):
+        for ch in range(2):
+            pieces = [placed(terms.at[i, ch], *numbers(k)[:2]) for i, k in enumerate(ks)]
+            for b in range(3):
+                piece = sum(p[b] for p in pieces[1:]) + pieces[0][b] if len(ks) > 1 else pieces[0][b]
                 acc[b, ch] = piece if first else acc[b, ch] + piece
 
     def peers(f):
@@ -492,9 +512,8 @@
     if len(rounds) > 1:
         next_round(1)
 
-    position(g, True)
-    add_terms(g, True)
-
+    chosen = (g, 1 - g) if G == 2 else (g,)
+    ahead(chosen)
     for i in range(2, len(rounds)):
         next_round(i)
     pair_copy(light_pair, light_pair, 0).wait()
@@ -506,18 +525,24 @@
     light_red = Reduce(p, light_mine, light_came, light_s)
     light_red.start()
 
-    def peer_position(j):
-        amp_copy(j, True).wait_recv()
-        k = lax.rem(g + G - j, G)
-        position(k, False)
-        if G > 2:
-            add_terms(k, False)
-
-    peers(peer_position)
+    if G == 2:
+        amp_copy(1, True).wait_recv()
+    behind(chosen, True)
+    if G > 2:
+        add_terms(chosen, True)
+
+        def peer_position(j):
+            amp_copy(j, True).wait_recv()
+            k = lax.rem(g + G - j, G)
+            ahead((k,))
+            behind((k,), False)
+            add_terms((k,), False)
+
+        peers(peer_position)
     grad_pairs = pair_copy(grad.at[:, p.rows(1 - p.h, p.s)], grad_pair, 1)
     grad_pairs.start()
-    if G == 2:
-        add_terms(1 - g, False)
+    if G <= 2:
+        add_terms(chosen, True)
     grad_pairs.wait()
     for j in range(p.owners):
         grad_mine[j] = (grad[:, p.chunk_rows(p.h, p.s, j), :]
@@ -600,7 +625,7 @@
             dma(4),
             vm(3, 2, rows, B),
             vm(blocks, W, B), vm(G, W, W), vm(G, 2, W, W),
-            vm(2, blocks, W + 2 * spare, B), vm(blocks, W + 2 * spare, B),
+            vm(2, 2 * W, W), vm(2, 2, blocks, W + 2 * spare, B), vm(blocks, W + 2 * spare, B),
             vm(3, 2, R, B), vm(3, R, B), vm(2, 2, R, B), vm(2, R, B),
             vm(W, W), vm(8, W), vm(p.part + 8, W),
             vm(p.owners, p.chunk + 8, W), vm(p.H - 1, p.chunk + 8, W),

time: 37.6 us -> 37 us (0.984)
  Pallas kernels: 34.9 us -> 34.3 us
    pallas_call x1, Pallas kernels: 34 us -> 33.4 us  [local(): pl.pallas_call(functools.partial(body, T, G), out_shape=(pltpu.VMEM(objec...]
where the time goes in v3:
time: 37 us; the launch traced here: 36.9 us
  Pallas kernels  34.3 us (93%)
  between operations  2.58 us (7%)
    pallas_call x1, Pallas kernels, local(): pl.pallas_call(functools.partial(body, T, G), out_shape=(pltpu.VMEM(objec...  33.4 us
    pallas_call x1, Pallas kernels, local(): pl.pallas_call(put, out_shape=(jax.ShapeDtypeStruct(object_field.shape, F...  0.87 us

profile of v3, /device:TPU:0, one launch (start us, length us, event | category | flops | bytes accessed | tf_op | source)
XLA Modules:
  0.0 36.9 jit_solution(17562139526063708681)
XLA Ops:
  2.6 33.4 %shard_map.86 = (f32[2,160,128]{2,1,0:T(8,128)S(1)}, f32[2,256,256]{2,1,0:T(8,128)S(1)}) custom-call(s32[1]{0:T(128)S(6)} %copy.9.row_in, s32[1]{0:T(128)S(6)} %copy.10.column_in, s32[1]{0:T(128)S(6)} %copy.11.live_in, f32[2,160,128]{2,1,0:T(8,128)} %obj.1, f32[2,256,256]{2,1,0:T(8,128)} %probe_in.1, f32[1,256,256]{2,1,0:T(8,128)} %amp.1, ...), custom_call_target="tpu_custom_call" | custom-call | tf_op jit(solution)/shard_map/pallas_call | solution.py:615
  36.0 0.9 %shard_map.87 = (f32[2,160,128]{2,1,0:T(8,128)}, f32[2,256,256]{2,1,0:T(8,128)}) custom-call(f32[2,160,128]{2,1,0:T(8,128)S(1)} %get-tuple-element.4.obj, f32[2,256,256]{2,1,0:T(8,128)S(1)} %get-tuple-element.5.probe), custom_call_target="tpu_custom_call" | custom-call | tf_op jit(solution)/shard_map/pallas_call | solution.py:643

commit v4 on v3

--- a/solution.py
+++ b/solution.py
@@ -56,16 +56,18 @@
     return mm(cat([head, tail, head], 1), cat([table[0], table[0], table[1]], 0))
 
 
-def fold_in(exits, tables):
+def rows_in(exits, tables):
     n = exits[0][0].shape[0] // 2
-    halves = []
-    for sign, table in ((1, tables[EVEN]), (-1, tables[ODD])):
-        halves.append(table_left(table, cat(
-            [cat([x[:n] + sign * x[n:] for x in parts], 0) for parts in exits], 1)))
+    return [table_left(table, cat([cat([x[:n] + sign * x[n:] for x in parts], 0) for parts in exits], 1))
+            for sign, table in ((1, tables[EVEN]), (-1, tables[ODD]))]
+
+
+def columns_in(halves, tables):
+    n = halves[0].shape[0] // 2
 
     def sides(sign):
         rows = []
-        for i in range(len(exits)):
+        for i in range(halves[0].shape[1] // (2 * n)):
             for y in halves:
                 y = y[:, 2 * n * i:2 * n * (i + 1)]
                 rows.append(cat([part[:, :n] + sign * part[:, n:] for part in (y[:n], y[n:])], 1))
@@ -74,21 +76,20 @@
     return table_right(sides(1), tables[EVEN_T]), table_right(sides(-1), tables[ODD_T])
 
 
-def fold_out(even, odd, tables):
-    n = even.shape[1] // 2
+def columns_out(even, odd, tables):
     e, o = table_right(even, tables[EVEN]), table_right(odd, tables[ODD])
-    plus, minus = e + o, e - o
-    count = even.shape[0] // (2 * n)
+    return e + o, e - o
+
+
+def rows_out(side, tables):
+    n = side.shape[1] // 2
     halves = []
     for q, table in ((0, tables[EVEN_T]), (1, tables[ODD_T])):
-        parts = []
-        for i in range(count):
-            r = slice((2 * i + q) * n, (2 * i + q + 1) * n)
-            parts.append(cat([cat([plus[r, :n], minus[r, :n]], 1), cat([plus[r, n:], minus[r, n:]], 1)], 0))
-        halves.append(table_left(table, cat(parts, 1)))
+        parts = [side[(2 * i + q) * n:(2 * i + q + 1) * n] for i in range(side.shape[0] // (2 * n))]
+        halves.append(table_left(table, cat([cat([x[:, :n], x[:, n:]], 0) for x in parts], 1)))
     plus, minus = halves[0] + halves[1], halves[0] - halves[1]
-    return [tuple(cat([side[part, 2 * n * i:2 * n * (i + 1)] for side in (plus, minus)], 0)
-                  for part in (slice(0, n), slice(n, 2 * n))) for i in range(count)]
+    return [tuple(cat([x[part, n * i:n * (i + 1)] for x in (plus, minus)], 0)
+                  for part in (slice(0, n), slice(n, 2 * n))) for i in range(plus.shape[1] // n)]
 
 
 def remote(src, dst, send, recv, tile, group):
@@ -103,9 +104,8 @@
         self.H = T // 2
         self.owners = self.H // 2 if self.H % 4 == 0 else self.H
         self.first = (self.H - self.owners) // 2
-        self.gs = max(n for n in range(1, G + 1) if G % n == 0 and n * self.owners * 8 <= W // 2)
-        self.W, self.half = W, W // 2
-        self.part = self.half // self.gs
+        self.gs = max(n for n in range(1, G + 1) if G % n == 0 and n * self.owners * 8 <= W)
+        self.part = W // self.gs
         self.chunk = self.part // self.owners
 
     def here(self, t, g):
@@ -117,11 +117,11 @@
         self.low = self.k < self.H // 2
         self.owner = jnp.logical_and(self.mine >= 0, self.mine < self.owners)
 
-    def rows(self, h, s):
-        return pl.ds(pl.multiple_of(h * self.half + s * self.part, 8), self.part)
-
-    def chunk_rows(self, h, s, j):
-        return pl.ds(pl.multiple_of(h * self.half + s * self.part + j * self.chunk, 8), self.chunk)
+    def rows(self, s):
+        return pl.ds(pl.multiple_of(s * self.part, 8), self.part)
+
+    def chunk_rows(self, s, j):
+        return pl.ds(pl.multiple_of(s * self.part + j * self.chunk, 8), self.chunk)
 
     def far_owner(self, i):
         return lax.rem(i + jnp.where(self.low, self.owners // 2, 0), self.owners)
@@ -239,13 +239,13 @@
 
 def body(T, G, row_in, column_in, live_in, obj, probe_in, amp, tables_in, new_obj, new_probe,
          scal_in, scal, probe, tables, load_sem, pad, amp_raw, amps, win, freq, terms, light_terms, acc,
-         acc_light, edge, edge_light, light_full, light_whole, light_pair, light_mine, light_came,
+         acc_light, edge, light_full, light_whole, light_pair, light_mine, light_came,
          grad, grad_pair, grad_mine, grad_came, full, reach, own_s, own_r, side_s, side_r, amp_s,
          amp_r, scal_s, edge_s, edge_r, pair_s, pair_r, light_s, grad_s, sent, line_r, group_r,
          relay_r):
     t, g = lax.axis_index("tile"), lax.axis_index("group")
     R, B = obj.shape[1:]
-    W = probe.shape[1]
+    W = probe.shape[2]
     rows = pad.shape[2]
     spare, blocks = rows - W, W // B
     p = Plan(T, G, W)
@@ -257,10 +257,12 @@
 
     own = pad.at[1, :, span(g)]
     loads = [pltpu.make_async_copy(src, dst, load_sem.at[i]) for i, (src, dst) in enumerate(
-        [(obj, own), (probe_in, probe), (tables_in, tables)])]
+        [(obj, own), (tables_in, tables)])]
     amp_loads = [pltpu.make_async_copy(amp.at[0, :, b * B:(b + 1) * B], amp_raw.at[b], load_sem.at[3])
                  for b in range(blocks)]
-    for load in amp_loads + loads:
+    probe_loads = [pltpu.make_async_copy(probe_in.at[:, :, b * B:(b + 1) * B], probe.at[:, b], load_sem.at[2])
+                   for b in range(blocks)]
+    for load in amp_loads + probe_loads + loads:
         load.start()
 
     barrier = pltpu.get_barrier_semaphore()
@@ -307,22 +309,18 @@
         return remote(slot, slot, amp_s.at[0], amp_r.at[j - 1], t, peer)
 
     def scal_copy(j):
-        return remote(scal_in, scal.at[g], scal_s.at[0], scal_s.at[1], t, lax.rem(g + j, G))
+        return remote(scal_in, scal.at[1, g], scal_s.at[0], scal_s.at[1], t, lax.rem(g + j, G))
+
+    def scal_side(right):
+        return remote(scal.at[1], scal.at[0 if right else 2], scal_s.at[2 + int(right)],
+                      scal_s.at[4 + int(right)], t + 1 if right else t - 1, g)
 
     def bytes_of(ref, send, recv):
         return remote(ref, ref, send, recv, p.partner, g)
 
-    def edge_copy(src, dst, right, base, arriving):
-        n = base + int(right)
-        side = dst.at[0 if right else 1]
-        if arriving:
-            return remote(side, side, edge_s.at[int(right)], edge_r.at[n], t - 1 if right else t + 1, g)
-        return remote(src.at[2 if right else 0], side, edge_s.at[int(right)], edge_r.at[n],
-                      t + 1 if right else t - 1, g)
-
-    def edges_sent(src, dst, base):
-        pl.when(not_first)(lambda: edge_copy(src, dst, False, base, False).wait_send())
-        pl.when(not_last)(lambda: edge_copy(src, dst, True, base, False).wait_send())
+    def edge_copy(right):
+        return remote(acc.at[2 if right else 0], edge.at[0 if right else 1], edge_s.at[int(right)],
+                      edge_r.at[int(right)], t + 1 if right else t - 1, g)
 
     def pair_copy(src, dst, n):
         return remote(src, dst, pair_s.at[n], pair_r.at[n], p.partner, g)
@@ -331,13 +329,13 @@
         pl.when(not_first)(lambda: to_side(ch, False, src, rows_of).start())
         pl.when(not_last)(lambda: to_side(ch, True, src, rows_of).start())
 
+    for j in range(1, G):
+        scal_copy(j).start()
     for ch in range(2):
         for q in range(len(pieces)):
             for j in range(1, G):
                 to_peer(j, ch, q, False).start()
         to_sides(ch, obj.at[ch], span(g))
-    for j in range(1, G):
-        scal_copy(j).start()
 
     known, rounds = 1, []
     while known < p.H - 1:
@@ -359,7 +357,7 @@
         pl.semaphore_wait(reach.at[i], below.astype(jnp.int32) + above.astype(jnp.int32))
 
     tell(0)
-    scal[g] = scal_in[...]
+    scal[1, g] = scal_in[...]
 
     pltpu.make_async_copy(amp_raw, amp_raw, load_sem.at[3]).wait()
     n = W // 2
@@ -378,45 +376,44 @@
     def _():
         pad[0] = jnp.zeros(pad.shape[1:], F32)
         edge[0] = jnp.zeros(edge.shape[1:], F32)
-        edge_light[0] = jnp.zeros(edge_light.shape[1:], F32)
+        scal[0] = jnp.zeros(scal.shape[1:], jnp.int32)
 
     @pl.when(t == T - 1)
     def _():
         pad[2] = jnp.zeros(pad.shape[1:], F32)
         edge[1] = jnp.zeros(edge.shape[1:], F32)
-        edge_light[1] = jnp.zeros(edge_light.shape[1:], F32)
+        scal[2] = jnp.zeros(scal.shape[1:], jnp.int32)
 
     terms[:, :, :, 0:spare] = jnp.zeros((2, 2, blocks, spare, B), F32)
     terms[:, :, :, spare + W:] = jnp.zeros((2, 2, blocks, spare, B), F32)
     light_terms[:, 0:spare] = jnp.zeros((blocks, spare, B), F32)
     light_terms[:, spare + W:] = jnp.zeros((blocks, spare, B), F32)
 
-    def hold(ref, value):
-        for b in range(blocks):
-            ref[b, spare:spare + W] = value[:, b * B:(b + 1) * B]
-
     for load in loads:
         load.wait()
+    pltpu.make_async_copy(probe, probe, load_sem.at[2]).wait()
     probe_light = probe[0] * probe[0] + probe[1] * probe[1]
-    hold(light_terms, probe_light)
+    light_terms[:, spare:spare + W] = probe_light
     light_max = jnp.max(probe_light) + 1e-06
 
+    if G > 1:
+        bytes_of(scal.at[1, 0:G - 1], scal_s.at[0], scal_s.at[1]).wait_recv()
+    pl.when(not_first)(lambda: scal_side(False).start())
+    pl.when(not_last)(lambda: scal_side(True).start())
     for ch in range(2):
         for q in range(len(pieces)):
             for j in range(1, G):
                 to_peer(j, ch, q, True).wait_recv()
                 rows_of = piece(lax.rem(g + G - j, G), q)
                 to_sides(ch, pad.at[1, ch, rows_of], rows_of)
-    if G > 1:
-        bytes_of(scal.at[0:G - 1], scal_s.at[0], scal_s.at[1]).wait_recv()
 
     def next_round(i):
         hear(i)
         if i + 1 < len(rounds):
             tell(i + 1)
 
-    def numbers(k):
-        return scal[k, 0, 0], scal[k, 1, 0], scal[k, 2, 0].astype(F32)
+    def numbers(k, side=1):
+        return scal[side, k, 0, 0], scal[side, k, 1, 0], scal[side, k, 2, 0].astype(F32)
 
     lane = lax.broadcasted_iota(jnp.int32, (8, B), 1)[0:1]
 
@@ -435,29 +432,37 @@
         stay = lane < B - column
         pieces = [pltpu.roll(pad[b, ch, pl.ds(row, W), :], shift, 1) for b in range(blocks + 1)]
         for b in range(blocks):
-            win[k, ch, :, b * B:(b + 1) * B] = jnp.where(stay, pieces[b], pieces[b + 1])
-
-    def place_light(k, first):
-        row, column, weight = numbers(k)
-        for b, piece in enumerate(placed(light_terms, row, column)):
-            piece = weight * piece
-            acc_light[b] = piece if first else acc_light[b] + piece
+            win[k, ch, b] = jnp.where(stay, pieces[b], pieces[b + 1])
+
+    def place_light(k):
+        total = None
+        for side in range(3):
+            row, column, weight = numbers(k, side)
+            piece = weight * placed(light_terms, row, column)[2 - side]
+            total = piece if total is None else total + piece
+        acc_light[...] += total
 
     def look(k, first):
         weight = numbers(k)[2]
         light = weight * (win[k, 0] * win[k, 0] + win[k, 1] * win[k, 1])
         light_full[...] = light if first else light_full[...] + light
 
-    def ahead(ks):
-        pr, pi = probe[0], probe[1]
+    def wide(ref):
+        return cat([ref[b] for b in range(blocks)], 1)
+
+    def begin(ks):
+        pr, pi = wide(probe.at[0]), wide(probe.at[1])
         exits = []
         for k in ks:
-            wr, wi = win[k, 0], win[k, 1]
+            wr, wi = wide(win.at[k, 0]), wide(win.at[k, 1])
             exits.append((pr * wr - pi * wi, pr * wi + pi * wr))
-        for q, value in enumerate(fold_in(exits, tables)):
-            freq[q, 0:len(ks) * W] = value
-
-    def behind(ks, first):
+        return rows_in(exits, tables)
+
+    def ahead(halves, count):
+        for q, value in enumerate(columns_in(halves, tables)):
+            freq[q, 0:count * W] = value
+
+    def behind(ks):
         scaled = []
         for q in range(2):
             rows = []
@@ -469,16 +474,20 @@
                     jnp.maximum(fr * fr + fi * fi, 0.0625))
                 rows.append(cat([fr * factor, fi * factor], 1))
             scaled.append(cat(rows, 0))
+        for c, value in enumerate(columns_out(*scaled, tables)):
+            freq[c, 0:len(ks) * W] = value
+
+    def end(ks, c, first):
         total = None
-        for i, (k, (mr, mi)) in enumerate(zip(ks, fold_out(*scaled, tables))):
-            wr, wi = win[k, 0], win[k, 1]
-            pr, pi = probe[0], probe[1]
+        for i, (k, (mr, mi)) in enumerate(zip(ks, rows_out(freq[c, 0:len(ks) * W], tables))):
+            wr, wi = win[k, 0, c], win[k, 1, c]
+            pr, pi = probe[0, c], probe[1, c]
             both = (wr * mr + wi * mi, wr * mi - wi * mr)
             total = both if total is None else [a + b for a, b in zip(total, both)]
-            hold(terms.at[i, 0], pr * mr + pi * mi)
-            hold(terms.at[i, 1], pr * mi - pi * mr)
+            terms[i, 0, c, spare:spare + W] = pr * mr + pi * mi
+            terms[i, 1, c, spare:spare + W] = pr * mi - pi * mr
         for ch in range(2):
-            grad[ch] = total[ch] if first else grad[ch] + total[ch]
+            grad[c, ch] = total[ch] if first else grad[c, ch] + total[ch]
 
     def add_terms(ks, first):
         for ch in range(2):
@@ -493,33 +502,37 @@
         elif G > 2:
             pl.loop(1, G)(f)
 
-    place_light(g, True)
-    peers(lambda j: place_light(lax.rem(g + G - j, G), False))
+    pl.when(not_last)(lambda: scal_side(False).wait_recv())
+    pl.when(not_first)(lambda: scal_side(True).wait_recv())
+    acc_light[...] = jnp.zeros(acc_light.shape, F32)
+    if G <= 2:
+        for k in range(G):
+            place_light(k)
+    else:
+        pl.loop(0, G)(place_light)
+    acc_light[...] = 1.0 / (acc_light[...] + 0.25 * light_max)
     next_round(0)
     for ch in range(2):
         pl.when(not_last)(lambda: side_bytes(pad.at[2, ch], ch, False).wait_recv())
         pl.when(not_first)(lambda: side_bytes(pad.at[0, ch], ch, True).wait_recv())
+    if len(rounds) > 1:
+        next_round(1)
     for ch in range(2):
         cut(g, ch)
         peers(lambda j: cut(lax.rem(g + G - j, G), ch))
     look(g, True)
     peers(lambda j: look(lax.rem(g + G - j, G), False))
-    light_whole[...] = jnp.sum(light_full[...].reshape(W // 8, 8, W), axis=0)
-    pair_copy(light_full.at[p.rows(1 - p.h, p.s)], light_pair.at[0:p.part], 0).start()
+    chosen = (g, 1 - g) if G == 2 else (g,)
+    light_whole[...] = jnp.sum(light_full[...].reshape(blocks * W // 8, 8, B), axis=0)
+    pair_copy(light_full.at[1 - p.h, p.rows(p.s)], light_pair.at[0:p.part], 0).start()
     pair_copy(light_whole, light_pair.at[p.part:p.part + 8], 0).start()
-    pl.when(not_first)(lambda: edge_copy(acc_light, edge_light, False, 0, False).start())
-    pl.when(not_last)(lambda: edge_copy(acc_light, edge_light, True, 0, False).start())
-    if len(rounds) > 1:
-        next_round(1)
-
-    chosen = (g, 1 - g) if G == 2 else (g,)
-    ahead(chosen)
+    ahead(begin(chosen), len(chosen))
     for i in range(2, len(rounds)):
         next_round(i)
     pair_copy(light_pair, light_pair, 0).wait()
     whole = light_whole[...] + light_pair[p.part:, :]
     for j in range(p.owners):
-        light_mine[j, 0:p.chunk] = (light_full[p.chunk_rows(p.h, p.s, j), :]
+        light_mine[j, 0:p.chunk] = (light_full[p.h, p.chunk_rows(p.s, j), :]
                                     + light_pair[j * p.chunk:(j + 1) * p.chunk, :])
         light_mine[j, p.chunk:] = whole
     light_red = Reduce(p, light_mine, light_came, light_s)
@@ -527,31 +540,37 @@
 
     if G == 2:
         amp_copy(1, True).wait_recv()
-    behind(chosen, True)
+    behind(chosen)
     if G > 2:
+        for c in range(blocks):
+            end(chosen, c, True)
         add_terms(chosen, True)
 
         def peer_position(j):
             amp_copy(j, True).wait_recv()
             k = lax.rem(g + G - j, G)
-            ahead((k,))
-            behind((k,), False)
+            ahead(begin((k,)), 1)
+            behind((k,))
+            for c in range(blocks):
+                end((k,), c, False)
             add_terms((k,), False)
 
         peers(peer_position)
-    grad_pairs = pair_copy(grad.at[:, p.rows(1 - p.h, p.s)], grad_pair, 1)
+    else:
+        end(chosen, 1 - p.h, True)
+    grad_pairs = pair_copy(grad.at[1 - p.h, :, p.rows(p.s)], grad_pair, 1)
     grad_pairs.start()
     if G <= 2:
+        end(chosen, p.h, True)
         add_terms(chosen, True)
     grad_pairs.wait()
     for j in range(p.owners):
-        grad_mine[j] = (grad[:, p.chunk_rows(p.h, p.s, j), :]
+        grad_mine[j] = (grad[p.h, :, p.chunk_rows(p.s, j), :]
                         + grad_pair[:, j * p.chunk:(j + 1) * p.chunk, :])
     grad_red = Reduce(p, grad_mine, grad_came, grad_s)
     grad_red.start()
-    edges_sent(acc_light, edge_light, 0)
-    pl.when(not_first)(lambda: edge_copy(acc, edge, False, 2, False).start())
-    pl.when(not_last)(lambda: edge_copy(acc, edge, True, 2, False).start())
+    pl.when(not_first)(lambda: edge_copy(False).start())
+    pl.when(not_last)(lambda: edge_copy(True).start())
 
     spread = Gather(p, full, grad_came, sent, line_r, group_r, relay_r)
 
@@ -560,32 +579,33 @@
         light = light_red.total()
         mean = jnp.sum(light[p.chunk:]) * (1.0 / (W * W))
         below = 1.0 / (light[:p.chunk] + 0.25 * mean + 1e-05)
-        here = p.chunk_rows(p.h, p.s, p.mine)
+        here = p.chunk_rows(p.s, p.mine)
         total = grad_red.total()
         for ch in range(2):
-            full[p.h, p.s, p.mine, ch] = probe[ch, here, :] - total[ch] * below
+            full[p.h, p.s, p.mine, ch] = probe[ch, p.h, here, :] - total[ch] * below
         spread.start()
 
     spread.forward()
-    for src, dst, base in ((acc_light, edge_light, 0), (acc, edge, 2)):
-        pl.when(not_last)(lambda: edge_copy(src, dst, False, base, True).wait_recv())
-        pl.when(not_first)(lambda: edge_copy(src, dst, True, base, True).wait_recv())
-    below = 1.0 / (acc_light[1] + edge_light[0] + edge_light[1] + 0.25 * light_max)
+    pl.when(not_last)(lambda: edge_copy(False).wait_recv())
+    pl.when(not_first)(lambda: edge_copy(True).wait_recv())
     for ch in range(2):
-        new_obj[ch] = own[ch] - (acc[1, ch] + edge[0, ch] + edge[1, ch]) * below
+        new_obj[ch] = own[ch] - (acc[1, ch] + edge[0, ch] + edge[1, ch]) * acc_light[...]
 
     if G > 1:
         bytes_of(pad.at[1, :, 0:(G - 1) * R], own_s.at[0], own_s.at[0]).wait_send()
         bytes_of(amps.at[0:G - 1], amp_s.at[0], amp_s.at[0]).wait_send()
-        bytes_of(scal.at[0:G - 1], scal_s.at[0], scal_s.at[1]).wait_send()
+        bytes_of(scal.at[1, 0:G - 1], scal_s.at[0], scal_s.at[1]).wait_send()
     pl.when(not_first)(lambda: side_bytes(pad.at[0], 0, False).wait_send())
     pl.when(not_last)(lambda: side_bytes(pad.at[0], 0, True).wait_send())
-    edges_sent(acc, edge, 2)
+    for right, there in ((False, not_first), (True, not_last)):
+        pl.when(there)(lambda: scal_side(right).wait_send())
+        pl.when(there)(lambda: edge_copy(right).wait_send())
     light_red.finish()
     grad_red.finish()
     spread.finish()
     for ch in range(2):
-        new_probe[ch] = full[:, :, :, ch].reshape(W, W)
+        for b in range(blocks):
+            new_probe[ch, :, b * B:(b + 1) * B] = full[b, :, :, ch].reshape(W, B)
     spread.drain()
 
 
@@ -619,21 +639,21 @@
         out_specs=(vmem, vmem),
         scratch_shapes=[
             pltpu.VMEM((8, 128), jnp.int32),
-            pltpu.VMEM((G, 8, 128), jnp.int32),
-            vm(2, W, W),
+            pltpu.VMEM((3, G, 8, 128), jnp.int32),
+            vm(2, blocks, W, B),
             pltpu.VMEM(tables.shape, BF16),
             dma(4),
             vm(3, 2, rows, B),
-            vm(blocks, W, B), vm(G, W, W), vm(G, 2, W, W),
+            vm(blocks, W, B), vm(G, W, W), vm(G, 2, blocks, W, B),
             vm(2, 2 * W, W), vm(2, 2, blocks, W + 2 * spare, B), vm(blocks, W + 2 * spare, B),
-            vm(3, 2, R, B), vm(3, R, B), vm(2, 2, R, B), vm(2, R, B),
-            vm(W, W), vm(8, W), vm(p.part + 8, W),
-            vm(p.owners, p.chunk + 8, W), vm(p.H - 1, p.chunk + 8, W),
-            vm(2, W, W), vm(2, p.part, W),
-            vm(p.owners, 2, p.chunk, W), vm(p.H - 1, 2, p.chunk, W),
-            vm(2, p.gs, p.owners, 2, p.chunk, W),
+            vm(3, 2, R, B), vm(R, B), vm(2, 2, R, B),
+            vm(blocks, W, B), vm(8, B), vm(p.part + 8, B),
+            vm(p.owners, p.chunk + 8, B), vm(p.H - 1, p.chunk + 8, B),
+            vm(blocks, 2, W, B), vm(2, p.part, B),
+            vm(p.owners, 2, p.chunk, B), vm(p.H - 1, 2, p.chunk, B),
+            vm(2, p.gs, p.owners, 2, p.chunk, B),
             pltpu.SemaphoreType.REGULAR((max((p.H - 2).bit_length(), 1),)),
-            dma(1), dma(4 * G - 4), dma(2), dma(4), dma(1), dma(G - 1), dma(2), dma(2), dma(4),
+            dma(1), dma(4 * G - 4), dma(2), dma(4), dma(1), dma(G - 1), dma(6), dma(2), dma(2),
             dma(2), dma(2), dma(2), dma(2), dma(3), dma(p.owners), dma((p.gs - 1) * p.owners), dma(1),
         ],
         compiler_params=pltpu.CompilerParams(

time: 37 us -> 36.7 us (level)
  Pallas kernels: 34.3 us -> 33.9 us
    pallas_call x1, Pallas kernels: 33.4 us -> 33 us  [local(): pl.pallas_call(functools.partial(body, T, G), out_shape=(pltpu.VMEM(objec...]
where the time goes in v4:
time: 36.7 us; the launch traced here: 36.5 us
  Pallas kernels  33.9 us (92%)
  between operations  2.58 us (7%)
    pallas_call x1, Pallas kernels, local(): pl.pallas_call(functools.partial(body, T, G), out_shape=(pltpu.VMEM(objec...  33 us
    pallas_call x1, Pallas kernels, local(): pl.pallas_call(put, out_shape=(jax.ShapeDtypeStruct(object_field.shape, F...  0.87 us

profile of v4, /device:TPU:0, one launch (start us, length us, event | category | flops | bytes accessed | tf_op | source)
XLA Modules:
  0.0 36.5 jit_solution(13627552791005025656)
XLA Ops:
  2.6 33.0 %shard_map.86 = (f32[2,160,128]{2,1,0:T(8,128)S(1)}, f32[2,256,256]{2,1,0:T(8,128)S(1)}) custom-call(s32[1]{0:T(128)S(6)} %copy.9.row_in, s32[1]{0:T(128)S(6)} %copy.10.column_in, s32[1]{0:T(128)S(6)} %copy.11.live_in, f32[2,160,128]{2,1,0:T(8,128)} %obj.1, f32[2,256,256]{2,1,0:T(8,128)} %probe_in.1, f32[1,256,256]{2,1,0:T(8,128)} %amp.1, ...), custom_call_target="tpu_custom_call" | custom-call | tf_op jit(solution)/shard_map/pallas_call | solution.py:635
  35.6 0.9 %shard_map.87 = (f32[2,160,128]{2,1,0:T(8,128)}, f32[2,256,256]{2,1,0:T(8,128)}) custom-call(f32[2,160,128]{2,1,0:T(8,128)S(1)} %get-tuple-element.4.obj, f32[2,256,256]{2,1,0:T(8,128)S(1)} %get-tuple-element.5.probe), custom_call_target="tpu_custom_call" | custom-call | tf_op jit(solution)/shard_map/pallas_call | solution.py:663

commit v5 on v4

--- a/solution.py
+++ b/solution.py
@@ -102,7 +102,7 @@
 class Plan:
     def __init__(self, T, G, W):
         self.H = T // 2
-        self.owners = self.H // 2 if self.H % 4 == 0 else self.H
+        self.owners = self.H
         self.first = (self.H - self.owners) // 2
         self.gs = max(n for n in range(1, G + 1) if G % n == 0 and n * self.owners * 8 <= W)
         self.part = W // self.gs
@@ -162,8 +162,7 @@
 
     def finish(self):
         p = self.p
-        pl.when(p.owner)(lambda: self.bytes_of(self.mine.at[0:p.owners - 1]).wait_send())
-        pl.when(jnp.logical_not(p.owner))(lambda: self.bytes_of(self.mine).wait_send())
+        self.bytes_of(self.mine.at[0:p.owners - 1]).wait_send()
 
 
 class Gather:

time: 36.7 us -> 36.3 us (0.989)
  no operation moved by 1% of the time
where the time goes in v5:
time: 36.3 us; the launch traced here: 36.1 us
  Pallas kernels  33.6 us (93%)
  between operations  2.58 us (7%)
    pallas_call x1, Pallas kernels, local(): pl.pallas_call(functools.partial(body, T, G), out_shape=(pltpu.VMEM(objec...  32.7 us
    pallas_call x1, Pallas kernels, local(): pl.pallas_call(put, out_shape=(jax.ShapeDtypeStruct(object_field.shape, F...  0.87 us

profile of v5, /device:TPU:0, one launch (start us, length us, event | category | flops | bytes accessed | tf_op | source)
XLA Modules:
  0.0 36.1 jit_solution(14721326157472147846)
XLA Ops:
  2.6 32.7 %shard_map.86 = (f32[2,160,128]{2,1,0:T(8,128)S(1)}, f32[2,256,256]{2,1,0:T(8,128)S(1)}) custom-call(s32[1]{0:T(128)S(6)} %copy.9.row_in, s32[1]{0:T(128)S(6)} %copy.10.column_in, s32[1]{0:T(128)S(6)} %copy.11.live_in, f32[2,160,128]{2,1,0:T(8,128)} %obj.1, f32[2,256,256]{2,1,0:T(8,128)} %probe_in.1, f32[1,256,256]{2,1,0:T(8,128)} %amp.1, ...), custom_call_target="tpu_custom_call" | custom-call | tf_op jit(solution)/shard_map/pallas_call | solution.py:634
  35.3 0.9 %shard_map.87 = (f32[2,160,128]{2,1,0:T(8,128)}, f32[2,256,256]{2,1,0:T(8,128)}) custom-call(f32[2,160,128]{2,1,0:T(8,128)S(1)} %get-tuple-element.4.obj, f32[2,256,256]{2,1,0:T(8,128)S(1)} %get-tuple-element.5.probe), custom_call_target="tpu_custom_call" | custom-call | tf_op jit(solution)/shard_map/pallas_call | solution.py:662

commit v6 on v5

--- a/solution.py
+++ b/solution.py
@@ -183,12 +183,11 @@
         slot = self.slot(p.h, p.s, j)
         return remote(slot, slot, self.sent.at[0], self.line.at[j], p.partner, p.g)
 
-    def group_copy(self, d, j, arriving):
+    def direct_arrival(self, d, j):
         p = self.p
         n = (d - 1) * p.owners + j
-        s = lax.rem(p.s + (p.gs - d if arriving else d), p.gs)
-        slot = self.slot(p.h, s if arriving else p.s, j)
-        return remote(slot, slot, self.sent.at[1], self.group.at[n], p.t, p.g - p.s + s)
+        slot = self.slot(p.h, lax.rem(p.s + p.gs - d, p.gs), j)
+        return remote(slot, slot, self.sent.at[1], self.group.at[n], p.partner, p.g)
 
     def relay_copy(self, d, j):
         p = self.p
@@ -198,16 +197,22 @@
     def bytes_of(self, ref, n):
         return remote(ref, ref, self.sent.at[n], self.relay.at[0], self.p.partner, self.p.g)
 
-    def hand_on(self, j):
-        for d in range(1, self.p.gs):
-            self.group_copy(d, j, False).start()
+    def hand_over(self, j):
         self.relay_copy(0, j).start()
 
+    def direct_copy(self, d, chip):
+        p = self.p
+        slot = self.slot(p.h, p.s, p.mine)
+        return remote(slot, slot, self.sent.at[1], self.group.at[(d - 1) * p.owners + p.mine],
+                      2 * chip + p.h, p.g - p.s + lax.rem(p.s + d, p.gs))
+
     def start(self):
         p = self.p
-        self.hand_on(p.mine)
+        self.hand_over(p.mine)
         for i in range(p.H):
             chip = p.far_chip(i)
+            for d in range(1, p.gs):
+                self.direct_copy(d, chip).start()
             pl.when(p.k != chip)(lambda: self.line_copy(chip).start())
 
     def forward(self):
@@ -218,11 +223,11 @@
             @pl.when(p.mine != j)
             def _():
                 self.line_arrival(j).wait_recv()
-                self.hand_on(j)
+                self.hand_over(j)
         for i in range(p.owners):
             for d in range(1, p.gs):
                 j = p.near_owner(i)
-                self.group_copy(d, j, True).wait_recv()
+                self.direct_arrival(d, j).wait_recv()
                 self.relay_copy(d, j).start()
 
     def finish(self):
@@ -528,6 +533,9 @@
     ahead(begin(chosen), len(chosen))
     for i in range(2, len(rounds)):
         next_round(i)
+    for d in range(1, p.gs):
+        pl.semaphore_signal(reach.at[len(rounds)], inc=1, device_id={
+            "tile": t, "group": g - p.s + lax.rem(p.s + d, p.gs)}, device_id_type=MESH)
     pair_copy(light_pair, light_pair, 0).wait()
     whole = light_whole[...] + light_pair[p.part:, :]
     for j in range(p.owners):
@@ -572,6 +580,9 @@
     pl.when(not_last)(lambda: edge_copy(True).start())
 
     spread = Gather(p, full, grad_came, sent, line_r, group_r, relay_r)
+
+    if p.gs > 1:
+        pl.semaphore_wait(reach.at[len(rounds)], p.gs - 1)
 
     @pl.when(p.owner)
     def _():
@@ -651,7 +662,7 @@
             vm(blocks, 2, W, B), vm(2, p.part, B),
             vm(p.owners, 2, p.chunk, B), vm(p.H - 1, 2, p.chunk, B),
             vm(2, p.gs, p.owners, 2, p.chunk, B),
-            pltpu.SemaphoreType.REGULAR((max((p.H - 2).bit_length(), 1),)),
+            pltpu.SemaphoreType.REGULAR(((p.H - 2).bit_length() + 1,)),
             dma(1), dma(4 * G - 4), dma(2), dma(4), dma(1), dma(G - 1), dma(6), dma(2), dma(2),
             dma(2), dma(2), dma(2), dma(2), dma(3), dma(p.owners), dma((p.gs - 1) * p.owners), dma(1),
         ],

time: 36.3 us -> 35.6 us (0.981)
  Pallas kernels: 33.6 us -> 32.9 us
    pallas_call x1, Pallas kernels: 32.7 us -> 32 us  [local(): pl.pallas_call(functools.partial(body, T, G), out_shape=(pltpu.VMEM(objec...]
where the time goes in v6:
time: 35.6 us; the launch traced here: 35.5 us
  Pallas kernels  32.9 us (92%)
  between operations  2.58 us (7%)
    pallas_call x1, Pallas kernels, local(): pl.pallas_call(functools.partial(body, T, G), out_shape=(pltpu.VMEM(objec...  32 us
    pallas_call x1, Pallas kernels, local(): pl.pallas_call(put, out_shape=(jax.ShapeDtypeStruct(object_field.shape, F...  0.87 us

profile of v6, /device:TPU:0, one launch (start us, length us, event | category | flops | bytes accessed | tf_op | source)
XLA Modules:
  0.0 35.5 jit_solution(13069589375168017330)
XLA Ops:
  2.6 32.0 %shard_map.86 = (f32[2,160,128]{2,1,0:T(8,128)S(1)}, f32[2,256,256]{2,1,0:T(8,128)S(1)}) custom-call(s32[1]{0:T(128)S(6)} %copy.9.row_in, s32[1]{0:T(128)S(6)} %copy.10.column_in, s32[1]{0:T(128)S(6)} %copy.11.live_in, f32[2,160,128]{2,1,0:T(8,128)} %obj.1, f32[2,256,256]{2,1,0:T(8,128)} %probe_in.1, f32[1,256,256]{2,1,0:T(8,128)} %amp.1, ...), custom_call_target="tpu_custom_call" | custom-call | tf_op jit(solution)/shard_map/pallas_call | solution.py:645
  34.6 0.9 %shard_map.87 = (f32[2,160,128]{2,1,0:T(8,128)}, f32[2,256,256]{2,1,0:T(8,128)}) custom-call(f32[2,160,128]{2,1,0:T(8,128)S(1)} %get-tuple-element.4.obj, f32[2,256,256]{2,1,0:T(8,128)S(1)} %get-tuple-element.5.probe), custom_call_target="tpu_custom_call" | custom-call | tf_op jit(solution)/shard_map/pallas_call | solution.py:673
